TPU v7x, 256 devices: a whole 4x4x8 slice. The times are simulated.
256 devices in a mesh: dp: 8 (over y, core), expert: 32 (over z, x).
Axes of the slice: x: 4, y: 4, z: 8, core: 2. Of those that a mesh axis runs over, the one named last changes fastest.
Arguments:
- tokens: bfloat16 [4096, 7168], P('expert', 'dp'), may hold values from -6 to 6
- cotangent: bfloat16 [4096, 7168], P('expert', 'dp'), may hold values from -6 to 6
- expert_ids: int32 [4096, 8], P('expert'), may hold values from 0 to 31, all different within a row; in each aligned block of 128 rows (0 to 127, 128 to 255, ...) at most 40 rows name the same one
- gates: float32 [4096, 8], P('expert'), may hold values from 0.05 to 0.5
- up_weight: bfloat16 [32, 7168, 1024], P('expert', 'dp'), may hold values from -0.0625 to 0.0625
- down_weight: bfloat16 [32, 1024, 7168], P('expert', None, 'dp'), may hold values from -0.1875 to 0.1875
Outputs:
- mixed: bfloat16 [4096, 7168], P('expert', 'dp')
- input_grads: bfloat16 [4096, 7168], P('expert', 'dp')
- up_grads: bfloat16 [32, 7168, 1024], P('expert', 'dp')
- down_grads: bfloat16 [32, 1024, 7168], P('expert', None, 'dp')
- gate_grads: float32 [4096, 8], P('expert')
Inputs may be any that keep to these rules, and one draw needn't show every extreme that they name: `expert_ids`: each row names 8 different experts. In the rows of one index of the expert axis no expert is named by more than 40 rows, a bound that some block reaches of them.
All inputs are finite; a program needn't handle non-finite values.
Results may differ from a plain program's by a relative error of at most 0.0064.
Values may be sent and summed in bfloat16 or wider, within the bound.
No kernel may reach another device: no remote copies, remote signals or barrier semaphores. Data moves between devices by JAX's collectives and lax.ppermute only.
A program may use at most 128 MiB of HBM per device.

v0:
```python
import jax
import jax.numpy as jnp
from jax import lax
from jax.experimental import pallas as pl
from jax.experimental.pallas import tpu as pltpu
from jax.sharding import Mesh
from jax.sharding import PartitionSpec as P

BF = jnp.bfloat16
F32 = jnp.float32

NZ, NX, NY = 8, 4, 4
CHUNKS = 4


ANY = pl.BlockSpec(memory_space=pl.ANY)
VMEM = pl.BlockSpec(memory_space=pltpu.VMEM)
SMEM = pl.BlockSpec(memory_space=pltpu.SMEM)


def swap(value, turn, apart=True):
    pairs = []
    for c in range(2):
        for i in range(NY):
            side = 1 if (i + (c if apart else 0) + turn) % 2 == 0 else -1
            pairs.append((2 * i + c, 2 * ((i + side) % NY) + c))
    return lax.ppermute(value, ("y", "core"), pairs)


def swap_core(value):
    return lax.ppermute(value, "core", [(0, 1), (1, 0)])


def tie(value, *others):
    return lax.optimization_barrier((value, *others))[0]


def scatter(rows):
    parts = rows.reshape(NZ * NX, rows.shape[0] // (NZ * NX), rows.shape[1])
    parts = lax.all_to_all(parts, ("z", "x"), split_axis=0, concat_axis=0, tiled=True)
    return parts.reshape(rows.shape)


def select_rows(pick, weights, values):
    slots, tok = pick.shape
    width = values.shape[1]
    step = slots // CHUNKS

    def kernel(pick_ref, *refs):
        weight_refs, (values_ref, out) = refs[: len(weights)], refs[len(weights) :]
        rows = jnp.dot(pick_ref[...], values_ref[...], preferred_element_type=F32)
        if weights:
            rows = rows * sum(
                jnp.sum(w[...].astype(F32), axis=1, keepdims=True) for w in weight_refs
            )
        out[...] = rows.astype(BF)

    chunk = pl.BlockSpec((step, tok), lambda k: (k, 0))
    return pl.pallas_call(
        kernel,
        grid=(CHUNKS,),
        out_shape=jax.ShapeDtypeStruct((slots, width), BF),
        in_specs=[chunk] * (1 + len(weights)) + [pl.BlockSpec((tok, width), lambda k: (0, 0))],
        out_specs=pl.BlockSpec((step, width), lambda k: (k, 0)),
        cost_estimate=pl.CostEstimate(flops=300_000_000, bytes_accessed=3_000_000, transcendentals=0),
        name="select_scaled" if weights else "select_plain",
    )(pick, *weights, values)


def mix_rows(picks, rows):
    slots, tok = picks[0].shape
    width = rows.shape[1]
    step = slots // CHUNKS

    def kernel(*refs):
        pick_refs, (rows_ref, out, total) = refs[: len(picks)], refs[len(picks) :]
        k = pl.program_id(0)
        part = None
        for ref in pick_refs:
            more = lax.dot_general(
                ref[...], rows_ref[...], (((0,), (0,)), ((), ())), preferred_element_type=F32
            )
            part = more if part is None else part + more

        @pl.when(k == 0)
        def _():
            total[...] = part

        @pl.when(k > 0)
        def _():
            total[...] += part

        @pl.when(k == CHUNKS - 1)
        def _():
            out[...] = total[...].astype(BF)

    return pl.pallas_call(
        kernel,
        grid=(CHUNKS,),
        out_shape=jax.ShapeDtypeStruct((tok, width), BF),
        in_specs=[pl.BlockSpec((step, tok), lambda k: (k, 0))] * len(picks)
        + [pl.BlockSpec((step, width), lambda k: (k, 0))],
        out_specs=pl.BlockSpec((tok, width), lambda k: (0, 0)),
        scratch_shapes=[pltpu.VMEM((tok, width), F32)],
        cost_estimate=pl.CostEstimate(
            flops=300_000_000 * len(picks), bytes_accessed=3_000_000, transcendentals=0
        ),
    )(*picks, rows)


def gate_terms(pick, rows, values):
    slots, tok = pick.shape
    width = rows.shape[1]
    step = slots // CHUNKS
    each = NZ * NX // CHUNKS
    cap = step // each

    def kernel(pick_ref, rows_ref, values_ref, out):
        chosen = jnp.dot(pick_ref[...], values_ref[...], preferred_element_type=F32)
        term = jnp.sum(chosen * rows_ref[...].astype(F32), axis=1, keepdims=True)
        placed = pick_ref[...].astype(F32) * term
        out[...] = jnp.concatenate(
            [
                jnp.sum(placed[n * cap : (n + 1) * cap], axis=0, keepdims=True)
                for n in range(each)
            ],
            axis=0,
        )

    return pl.pallas_call(
        kernel,
        grid=(CHUNKS,),
        out_shape=jax.ShapeDtypeStruct((NZ * NX, tok), F32),
        in_specs=[
            pl.BlockSpec((step, tok), lambda k: (k, 0)),
            pl.BlockSpec((step, width), lambda k: (k, 0)),
            pl.BlockSpec((tok, width), lambda k: (0, 0)),
        ],
        out_specs=pl.BlockSpec((each, tok), lambda k: (k, 0)),
        cost_estimate=pl.CostEstimate(flops=300_000_000, bytes_accessed=3_000_000, transcendentals=0),
        name="gate_terms",
    )(pick, rows, values)


def partial_sums(table, slot_rows, weight, contract):
    slots, width = slot_rows.shape
    rows = slots // (2 * NY)
    hid = weight.shape[1 - contract]
    step = 256

    def kernel(table_ref, weight_ref, rows_ref, keep, away, held, sems):
        first = pl.program_id(0) == 0
        core = table_ref[4 * NY]

        def get(i, h):
            return pltpu.make_async_copy(
                rows_ref.at[i, h ^ core], held.at[pl.ds((2 * i + h) * rows, rows)], sems.at[i, h]
            )

        @pl.when(first)
        def _():
            for i in range(NY):
                for h in range(2):
                    get(i, h).start()

        for i in range(NY):
            at = i * 2 * rows

            @pl.when(first)
            def _():
                for h in range(2):
                    get(i, h).wait()

            made = lax.dot_general(
                held[at : at + 2 * rows], weight_ref[...], (((1,), (contract,)), ((), ())),
                preferred_element_type=F32,
            )
            keep[table_ref[i]] = made[:rows]
            away[table_ref[NY + i]] = made[rows:].astype(BF)

    if contract == 0:
        weight_spec = pl.BlockSpec((width, step), lambda n: (0, n))
    else:
        weight_spec = pl.BlockSpec((step, width), lambda n: (n, 0))
    out_spec = pl.BlockSpec((NY, rows, step), lambda n: (0, 0, n))
    return pl.pallas_call(
        kernel,
        grid=(hid // step,),
        out_shape=[
            jax.ShapeDtypeStruct((NY, rows, hid), F32), jax.ShapeDtypeStruct((NY, rows, hid), BF)
        ],
        in_specs=[SMEM, weight_spec, ANY],
        out_specs=[out_spec] * 2,
        scratch_shapes=[pltpu.VMEM((slots, width), BF), pltpu.SemaphoreType.DMA((NY, 2))],
        cost_estimate=pl.CostEstimate(
            flops=2_400_000_000, bytes_accessed=9_000_000, transcendentals=0
        ),
    )(table, weight, slot_rows.reshape(NY, 2, rows, width))


def expand_rows(table, shares, weight, contract):
    rows = shares[0].shape[1]
    hid, width = weight.shape[contract], weight.shape[1 - contract]

    def kernel(table_ref, weight_ref, *refs):
        ins, (out, joined, held, made, held_weight, in_sems, out_sems, join_sems, weight_sem) = (
            refs[:4], refs[4:]
        )
        core = table_ref[4 * NY]
        fetch = pltpu.make_async_copy(weight_ref, held_weight, weight_sem)
        fetch.start()
        for n in range(4):
            for m in range(2):
                place = table_ref[2 * NY + 2 * n + m]
                half = core if n < 2 else 1 - core
                pltpu.make_async_copy(
                    ins[n].at[m], held.at[place, half], in_sems.at[place, half]
                ).start()

        def put(i):
            return pltpu.make_async_copy(made.at[i], out.at[i], out_sems.at[i])

        def keep(i):
            return pltpu.make_async_copy(held.at[i], joined.at[i], join_sems.at[i])

        fetch.wait()

        def step(i, carry):
            for h in range(2):
                pltpu.make_async_copy(ins[0].at[0], held.at[i, h], in_sems.at[i, h]).wait()
            keep(i).start()
            made[i] = lax.dot_general(
                held[i].reshape(2 * rows, hid), held_weight[...],
                (((1,), (contract,)), ((), ())), preferred_element_type=F32,
            ).astype(BF)
            put(i).start()
            return carry

        lax.fori_loop(0, NY, step, 0)
        for i in range(NY):
            put(i).wait()
            keep(i).wait()

    out, joined = pl.pallas_call(
        kernel,
        out_shape=[
            jax.ShapeDtypeStruct((NY, 2 * rows, width), BF),
            jax.ShapeDtypeStruct((NY, 2, rows, hid), BF),
        ],
        in_specs=[SMEM, ANY] + [ANY] * 4,
        out_specs=[ANY] * 2,
        scratch_shapes=[
            pltpu.VMEM((NY, 2, rows, hid), BF),
            pltpu.VMEM((NY, 2 * rows, width), BF),
            pltpu.VMEM(weight.shape, BF),
            pltpu.SemaphoreType.DMA((NY, 2)),
            pltpu.SemaphoreType.DMA((NY,)),
            pltpu.SemaphoreType.DMA((NY,)),
            pltpu.SemaphoreType.DMA,
        ],
        cost_estimate=pl.CostEstimate(
            flops=2_400_000_000, bytes_accessed=9_000_000, transcendentals=0
        ),
    )(table, weight, *shares)
    return out.reshape(NY * 2 * rows, width), joined.reshape(NY * 2 * rows, hid)


def weight_grads(left, right, step):
    slots, count = left.shape
    width = right.shape[1]

    def kernel(left_ref, right_ref, out):
        out[...] = lax.dot_general(
            left_ref[...], right_ref[...], (((0,), (0,)), ((), ())), preferred_element_type=F32
        ).astype(BF)

    return pl.pallas_call(
        kernel,
        grid=(count // step,),
        out_shape=jax.ShapeDtypeStruct((count, width), BF),
        in_specs=[
            pl.BlockSpec((slots, step), lambda n: (0, n)),
            pl.BlockSpec((slots, width), lambda n: (0, 0)),
        ],
        out_specs=pl.BlockSpec((step, width), lambda n: (n, 0)),
        cost_estimate=pl.CostEstimate(
            flops=2_400_000_000, bytes_accessed=7_000_000, transcendentals=0
        ),
    )(left, right)


def route_kernel(ids_ref, gates_ref, tokens_ref, pick_ref, hi_ref, lo_ref, rows_ref):
    tok = ids_ref.shape[1]
    each = 8
    cap = pick_ref.shape[0] // each
    chosen, weight = [], []
    for n in range(each):
        hit = jnp.where(ids_ref[...] == pl.program_id(0) * each + n, 1.0, 0.0)
        chosen.append(jnp.sum(hit, axis=0, keepdims=True))
        weight.append(jnp.sum(hit * gates_ref[...], axis=0, keepdims=True))
    chosen = jnp.concatenate(chosen, axis=0)
    earlier = lax.broadcasted_iota(jnp.int32, (tok, tok), 0)
    later = lax.broadcasted_iota(jnp.int32, (tok, tok), 1)
    strict = jnp.where(earlier < later, 1.0, 0.0).astype(BF)
    rank = jnp.dot(chosen.astype(BF), strict, preferred_element_type=F32)
    place = jnp.where(chosen > 0.0, rank, -1.0)
    slot = lax.broadcasted_iota(jnp.int32, (cap, tok), 0).astype(F32)
    one, high, low = [], [], []
    for n in range(each):
        here = slot == place[n : n + 1]
        gate = jnp.where(here, jnp.broadcast_to(weight[n], (cap, tok)), 0.0)
        one.append(jnp.where(here, 1.0, 0.0))
        high.append(gate.astype(BF).astype(F32))
        low.append(gate - high[-1])
    pick = jnp.concatenate(one, axis=0).astype(BF)
    pick_ref[...] = pick
    rows_ref[...] = jnp.dot(pick, tokens_ref[...], preferred_element_type=F32).astype(BF)
    hi_ref[...] = jnp.concatenate(high, axis=0).astype(BF)
    lo_ref[...] = jnp.concatenate(low, axis=0).astype(BF)


def grad_share(keep, got, near, last, pre):
    rows, hid = pre.shape
    step = 16

    def kernel(keep_ref, got_ref, near_ref, last_ref, pre_ref, out):
        def body(n, carry):
            at = pl.ds(pl.multiple_of(n * step, step), step)
            raw = keep_ref[0, at].astype(F32) + got_ref[0, at].astype(F32)
            raw = raw + near_ref[0, at].astype(F32) + last_ref[at].astype(F32)
            pre = pre_ref[at]
            logistic = 1.0 / (1.0 + jnp.exp(-pre))
            out[at] = (raw * (logistic * (1.0 + pre * (1.0 - logistic)))).astype(BF)
            return carry

        lax.fori_loop(0, rows // step, body, 0)

    return pl.pallas_call(
        kernel,
        grid=(1,),
        out_shape=jax.ShapeDtypeStruct((rows, hid), BF),
        in_specs=[
            pl.BlockSpec((1, rows, hid), lambda n: (2, 0, 0)),
            pl.BlockSpec((1, rows, hid), lambda n: (2, 0, 0)),
            pl.BlockSpec((1, rows, hid), lambda n: (0, 0, 0)),
            pl.BlockSpec((rows, hid), lambda n: (0, 0)),
            pl.BlockSpec((rows, hid), lambda n: (0, 0)),
        ],
        out_specs=pl.BlockSpec((rows, hid), lambda n: (0, 0)),
        cost_estimate=pl.CostEstimate(flops=3_000_000, bytes_accessed=3_000_000, transcendentals=200_000),
        name="grad_share",
    )(keep, got, near, last, pre)


def per_device(tokens, cotangent, expert_ids, gates, up_weight, down_weight):
    tok, width = tokens.shape
    top = expert_ids.shape[1]
    experts = NZ * NX
    cap = tok * top * 5 // (4 * experts)
    slots = experts * cap
    y, core = lax.axis_index("y"), lax.axis_index("core")
    w_up, w_down = up_weight[0], down_weight[0]

    side_y = 1 - 2 * ((y + core) % 2)
    turn = (jnp.arange(NY, dtype=jnp.int32) - y) % NY

    def share_at(side, places):
        near = jnp.where(turn == side % NY, places[1], places[2])
        return jnp.where(turn == 0, places[0], jnp.where(turn == 2, places[3], near))

    def gathered(side):
        return (y + jnp.stack([0 * side, side, -side, 0 * side + 2])) % NY

    table = jnp.concatenate([
        share_at(side_y, (2, 0, 3, 1)),
        share_at(-side_y, (2, 0, 3, 1)),
        gathered(side_y),
        gathered(-side_y),
        core[None],
    ]).astype(jnp.int32)

    ids_t, gates_t = expert_ids.T, gates.T
    routing = pl.BlockSpec((slots // 4, tok), lambda k: (k, 0))
    small = pl.BlockSpec((top, tok), lambda k: (0, 0))
    pick, gate_hi, gate_lo, x_rows = pl.pallas_call(
        route_kernel,
        grid=(4,),
        out_shape=[jax.ShapeDtypeStruct((slots, tok), BF)] * 3
        + [jax.ShapeDtypeStruct((slots, width), BF)],
        in_specs=[small, small, pl.BlockSpec((tok, width), lambda k: (0, 0))],
        out_specs=[routing] * 3 + [pl.BlockSpec((slots // 4, width), lambda k: (k, 0))],
        name="route",
    )(ids_t, gates_t, tokens)

    def reduce(keep, away):
        got = swap_core(away)
        first = (keep[:2] + got[:2].astype(F32)).astype(BF)
        near = swap(first, 0)
        second = (keep[3] + got[3].astype(F32) + near[1].astype(F32)).astype(BF)
        return got, near, swap(second, 1), first

    def spread(share):
        pair = jnp.stack([share, swap(share, 0)])
        other_pair = swap_core(pair)
        far = swap(pair, 1)
        other_far = swap_core(far)
        return [pair, far, other_pair, other_far]

    x_slots = scatter(x_rows)
    g_slots = scatter(tie(select_rows(pick, (gate_hi, gate_lo), cotangent), x_slots))

    keep, away = partial_sums(table, x_slots, w_up, 0)
    got, near, last, _ = reduce(keep, away)
    pre = keep[2] + got[2].astype(F32) + near[0].astype(F32) + last.astype(F32)
    hidden_shares = spread((pre * jax.nn.sigmoid(pre)).astype(BF))

    keep, away = partial_sums(table, tie(g_slots, hidden_shares[1]), w_down, 1)
    got, near, last, first = reduce(keep, away)
    hidden_shares[0] = tie(hidden_shares[0], keep)
    out_rows, hidden = expand_rows(table, hidden_shares, w_down, 0)
    out_back = scatter(tie(out_rows, first))

    grads = spread(grad_share(keep, got, near, last, pre))
    dx_rows, pre_grad = expand_rows(table, grads, w_up, 1)
    dx_back = scatter(tie(dx_rows, out_back))

    mixed = mix_rows((gate_hi, gate_lo), out_back)
    terms = gate_terms(pick, tie(out_back, dx_rows), cotangent)
    terms = terms + swap_core(terms)
    terms = terms + swap(terms, 0, False)
    terms = terms + swap(terms, 1, False)
    own = ids_t[:, None, :] == jnp.arange(experts, dtype=jnp.int32)[None, :, None]
    gate_grads = jnp.sum(jnp.where(own, terms[None], 0.0), axis=1).T
    down_grad = weight_grads(tie(hidden, dx_rows), g_slots, 256)
    up_grad = weight_grads(x_slots, pre_grad, 128)
    input_grads = mix_rows((pick,), tie(dx_back, down_grad, up_grad, mixed))
    return mixed, input_grads, up_grad[None], down_grad[None], gate_grads


def solution(mesh):
    grid = Mesh(mesh.devices.reshape(NY, 2, NZ, NX), ("y", "core", "z", "x"))
    dp, ex = ("y", "core"), ("z", "x")
    return jax.shard_map(
        per_device,
        mesh=grid,
        in_specs=(P(ex, dp), P(ex, dp), P(ex, None), P(ex, None), P(ex, dp, None), P(ex, None, dp)),
        out_specs=(P(ex, dp), P(ex, dp), P(ex, dp, None), P(ex, None, dp), P(ex, None)),
        check_vma=False,
    )
```

profile of v0, /device:TPU:24, one launch (start us, length us, event | category | flops | bytes accessed | tf_op | source)
XLA Modules:
  0.0 292.8 jit_solution(16926963377612617170)
XLA Ops:
  4.6 11.3 %all-to-all-start = ((bf16[32,40,896]{2,1,0:T(8,128)(2,1)}), bf16[32,40,896]{2,1,0:T(8,128)(2,1)S(1)}, u32[]{:S(2)}, u32[]{:S(2)}) async-start(bf16[32,40,896]{2,1,0:T(8,128)(2,1)} %bitcast.40), calls=%async_computation | async-start | bytes 4587520 | tf_op jit(solution)/shard_map/all_to_all | solution.py:40
  16.7 4.4 %select_scaled.1 = bf16[1280,896]{1,0:T(8,128)(2,1)} custom-call(bf16[1280,128]{1,0:T(8,128)(2,1)} %get-tuple-element.30.pick_ref.refs_0_, bf16[1280,128]{1,0:T(8,128)(2,1)} %get-tuple-element.25.refs_0_, bf16[1280,128]{1,0:T(8,128)(2,1)} %get-tuple-element.26.refs_1_, bf16[128,896]{1,0:T(8,128)(2,1)} %values_ref.1), custom_call_target="tpu_custom_call" | custom-call | flops 300000000 | bytes 3000000 | tf_op jit(solution)/shard_map/select_scaled/pallas_call | solution.py:59
  21.1 49.2 %all-to-all-done = bf16[32,40,896]{2,1,0:T(8,128)(2,1)S(1)} async-done(((bf16[32,40,896]{2,1,0:T(8,128)(2,1)}), bf16[32,40,896]{2,1,0:T(8,128)(2,1)S(1)}, u32[]{:S(2)}, u32[]{:S(2)}) %all-to-all-start) | async-done | bytes 2293792 | tf_op jit(solution)/shard_map/all_to_all | solution.py:40
  71.7 5.5 %all-to-all-start.1 = ((bf16[32,40,896]{2,1,0:T(8,128)(2,1)}), bf16[32,40,896]{2,1,0:T(8,128)(2,1)}, u32[]{:S(2)}, u32[]{:S(2)}) async-start(bf16[32,40,896]{2,1,0:T(8,128)(2,1)} %bitcast.37), calls=%async_computation.1 | async-start | bytes 4587520 | tf_op jit(solution)/shard_map/all_to_all | solution.py:40
  77.2 11.0 %shard_map.101 = (f32[4,160,1024]{2,1,0:T(8,128)}, bf16[4,160,1024]{2,1,0:T(8,128)(2,1)}) custom-call(s32[17]{0:T(128)} %concatenate.3.table_ref, bf16[896,1024]{1,0:T(8,128)(2,1)} %bitcast.53, bf16[4,2,160,896]{3,2,1,0:T(8,128)(2,1)} %bitcast.38), custom_call_target="tpu_custom_call" | custom-call | flops 2400000000 | bytes 9000000 | tf_op jit(solution)/shard_map/pallas_call | solution.py:186
  94.0 9.8 %collective-permute-done.1 = bf16[2,160,1024]{2,1,0:T(8,128)(2,1)S(1)} collective-permute-done((bf16[2,160,1024]{2,1,0:T(8,128)(2,1)S(1)}, bf16[2,160,1024]{2,1,0:T(8,128)(2,1)S(1)}, u32[]{:S(2)}, u32[]{:S(2)}) %collective-permute-start.1) | collective-permute-done | bytes 655392 | tf_op jit(solution)/shard_map/ppermute | solution.py:27
  104.3 8.1 %collective-permute-done.2 = bf16[160,1024]{1,0:T(8,128)(2,1)S(1)} collective-permute-done((bf16[160,1024]{1,0:T(8,128)(2,1)S(1)}, bf16[160,1024]{1,0:T(8,128)(2,1)S(1)}, u32[]{:S(2)}, u32[]{:S(2)}) %collective-permute-start.2) | collective-permute-done | bytes 327712 | tf_op jit(solution)/shard_map/ppermute | solution.py:27
  113.4 7.1 %collective-permute-done.3 = bf16[160,1024]{1,0:T(8,128)(2,1)S(1)} collective-permute-done((bf16[160,1024]{1,0:T(8,128)(2,1)S(1)}, bf16[160,1024]{1,0:T(8,128)(2,1)S(1)}, u32[]{:S(2)}, u32[]{:S(2)}) %collective-permute-start.3) | collective-permute-done | bytes 327712 | tf_op jit(solution)/shard_map/ppermute | solution.py:27
  120.9 11.7 %collective-permute-done.4.refs_1_ = bf16[2,160,1024]{2,1,0:T(8,128)(2,1)} collective-permute-done((bf16[2,160,1024]{2,1,0:T(8,128)(2,1)S(1)}, bf16[2,160,1024]{2,1,0:T(8,128)(2,1)}, u32[]{:S(2)}, u32[]{:S(2)}) %collective-permute-start.4) | collective-permute-done | bytes 655392 | tf_op jit(solution)/shard_map/ppermute | solution.py:27
  132.6 11.5 %shard_map.102 = (f32[4,160,1024]{2,1,0:T(8,128)}, bf16[4,160,1024]{2,1,0:T(8,128)(2,1)}) custom-call(s32[17]{0:T(128)} %concatenate.3.table_ref, bf16[1024,896]{1,0:T(8,128)(2,1)} %bitcast.51, bf16[4,2,160,896]{3,2,1,0:T(8,128)(2,1)} %bitcast.16.rows_ref), custom_call_target="tpu_custom_call" | custom-call | flops 2400000000 | bytes 9000000 | tf_op jit(solution)/shard_map/pallas_call | solution.py:186
  149.4 7.2 %shard_map.103 = (bf16[4,320,896]{2,1,0:T(8,128)(2,1)}, bf16[4,2,160,1024]{3,2,1,0:T(8,128)(2,1)}) custom-call(s32[17]{0:T(128)} %concatenate.3.table_ref, bf16[1024,896]{1,0:T(8,128)(2,1)} %bitcast.52, bf16[2,160,1024]{2,1,0:T(8,128)(2,1)} %copy-done.5, bf16[2,160,1024]{2,1,0:T(8,128)(2,1)} %collective-permute-done.4.refs_1_, ...), custom_call_target="tpu_custom_call" | custom-call | flops 2400000000 | bytes 9000000 | tf_op jit(solution)/shard_map/pallas_call | solution.py:244
  158.8 9.7 %all-to-all-start.2 = ((bf16[32,40,896]{2,1,0:T(8,128)(2,1)}), bf16[32,40,896]{2,1,0:T(8,128)(2,1)S(1)}, u32[]{:S(2)}, u32[]{:S(2)}) async-start(bf16[32,40,896]{2,1,0:T(8,128)(2,1)} %bitcast.41), calls=%async_computation.2 | async-start | bytes 4587520 | tf_op jit(solution)/shard_map/all_to_all | solution.py:40
  168.6 10.8 %collective-permute-done.8.near_ref = bf16[2,160,1024]{2,1,0:T(8,128)(2,1)S(1)} collective-permute-done((bf16[2,160,1024]{2,1,0:T(8,128)(2,1)}, bf16[2,160,1024]{2,1,0:T(8,128)(2,1)S(1)}, u32[]{:S(2)}, u32[]{:S(2)}) %collective-permute-start.8) | collective-permute-done | bytes 655392 | tf_op jit(solution)/shard_map/ppermute | solution.py:27
  181.3 8.1 %collective-permute-done.9.last_ref = bf16[160,1024]{1,0:T(8,128)(2,1)S(1)} collective-permute-done((bf16[160,1024]{1,0:T(8,128)(2,1)S(1)}, bf16[160,1024]{1,0:T(8,128)(2,1)S(1)}, u32[]{:S(2)}, u32[]{:S(2)}) %collective-permute-start.9) | collective-permute-done | bytes 327712 | tf_op jit(solution)/shard_map/ppermute | solution.py:27
  192.8 7.3 %collective-permute-done.10 = bf16[160,1024]{1,0:T(8,128)(2,1)S(1)} collective-permute-done((bf16[160,1024]{1,0:T(8,128)(2,1)}, bf16[160,1024]{1,0:T(8,128)(2,1)S(1)}, u32[]{:S(2)}, u32[]{:S(2)}) %collective-permute-start.10) | collective-permute-done | bytes 327712 | tf_op jit(solution)/shard_map/ppermute | solution.py:27
  201.7 11.6 %collective-permute-done.11.refs_1_ = bf16[2,160,1024]{2,1,0:T(8,128)(2,1)S(1)} collective-permute-done((bf16[2,160,1024]{2,1,0:T(8,128)(2,1)S(1)}, bf16[2,160,1024]{2,1,0:T(8,128)(2,1)S(1)}, u32[]{:S(2)}, u32[]{:S(2)}) %collective-permute-start.11) | collective-permute-done | bytes 655392 | tf_op jit(solution)/shard_map/ppermute | solution.py:27
  215.5 7.4 %shard_map.105 = (bf16[4,320,896]{2,1,0:T(8,128)(2,1)}, bf16[4,2,160,1024]{3,2,1,0:T(8,128)(2,1)}) custom-call(s32[17]{0:T(128)} %concatenate.3.table_ref, bf16[896,1024]{1,0:T(8,128)(2,1)} %bitcast.54, bf16[2,160,1024]{2,1,0:T(8,128)(2,1)} %copy-done.6, bf16[2,160,1024]{2,1,0:T(8,128)(2,1)} %copy-done.10, bf16[2,160,1024]{2,1,0:T(8,128)(2,1)} %copy-done.11, ...), custom_call_target="tpu_custom_call" | custom-call | flops 2400000000 | bytes 9000000 | tf_op jit(solution)/shard_map/pallas_call | solution.py:244
  224.5 9.6 %all-to-all-start.3 = ((bf16[32,40,896]{2,1,0:T(8,128)(2,1)}), bf16[32,40,896]{2,1,0:T(8,128)(2,1)}, u32[]{:S(2)}, u32[]{:S(2)}) async-start(bf16[32,40,896]{2,1,0:T(8,128)(2,1)} %bitcast.42), calls=%async_computation.3 | async-start | bytes 4587520 | tf_op jit(solution)/shard_map/all_to_all | solution.py:40
  234.1 4.3 %gate_terms.1 = f32[32,128]{1,0:T(8,128)} custom-call(bf16[1280,128]{1,0:T(8,128)(2,1)} %get-tuple-element.30.pick_ref.refs_0_, bf16[1280,896]{1,0:T(8,128)(2,1)} %bitcast.35, bf16[128,896]{1,0:T(8,128)(2,1)} %values_ref.1), custom_call_target="tpu_custom_call" | custom-call | flops 300000000 | bytes 3000000 | tf_op jit(solution)/shard_map/gate_terms/pallas_call | solution.py:130
  238.4 8.0 %shard_map.107 = bf16[896,1024]{1,0:T(8,128)(2,1)} custom-call(bf16[1280,896]{1,0:T(8,128)(2,1)} %bitcast.39, bf16[1280,1024]{1,0:T(8,128)(2,1)} %bitcast.56), custom_call_target="tpu_custom_call" | custom-call | flops 2400000000 | bytes 7000000 | tf_op jit(solution)/shard_map/pallas_call | solution.py:277
  246.6 6.6 %shard_map.106 = bf16[1024,896]{1,0:T(8,128)(2,1)} custom-call(bf16[1280,1024]{1,0:T(8,128)(2,1)} %bitcast.55, bf16[1280,896]{1,0:T(8,128)(2,1)} %bitcast.15.right_ref), custom_call_target="tpu_custom_call" | custom-call | flops 2400000000 | bytes 7000000 | tf_op jit(solution)/shard_map/pallas_call | solution.py:277
  253.5 4.6 %shard_map.104 = bf16[128,896]{1,0:T(8,128)(2,1)} custom-call(bf16[1280,128]{1,0:T(8,128)(2,1)} %get-tuple-element.25.refs_0_, bf16[1280,128]{1,0:T(8,128)(2,1)} %get-tuple-element.26.refs_1_, bf16[1280,896]{1,0:T(8,128)(2,1)} %bitcast.36), custom_call_target="tpu_custom_call" | custom-call | flops 600000000 | bytes 3000000 | tf_op jit(solution)/shard_map/pallas_call | solution.py:97
  258.9 29.9 %all-to-all-done.3 = bf16[32,40,896]{2,1,0:T(8,128)(2,1)} async-done(((bf16[32,40,896]{2,1,0:T(8,128)(2,1)}), bf16[32,40,896]{2,1,0:T(8,128)(2,1)}, u32[]{:S(2)}, u32[]{:S(2)}) %all-to-all-start.3) | async-done | bytes 2293792 | tf_op jit(solution)/shard_map/all_to_all | solution.py:40
  288.7 4.1 %shard_map.108 = bf16[128,896]{1,0:T(8,128)(2,1)} custom-call(bf16[1280,128]{1,0:T(8,128)(2,1)} %get-tuple-element.30.pick_ref.refs_0_, bf16[1280,896]{1,0:T(8,128)(2,1)} %bitcast.25.refs_1_), custom_call_target="tpu_custom_call" | custom-call | flops 300000000 | bytes 3000000 | tf_op jit(solution)/shard_map/pallas_call | solution.py:97
  (70 shorter events, 33.3 us)
Async XLA Ops:
  4.6 65.6 %all-to-all-start = ((bf16[32,40,896]{2,1,0:T(8,128)(2,1)}), bf16[32,40,896]{2,1,0:T(8,128)(2,1)S(1)}, u32[]{:S(2)}, u32[]{:S(2)}) async-start(bf16[32,40,896]{2,1,0:T(8,128)(2,1)} %bitcast.40), calls=%async_computation | async-start | bytes 4587520 | tf_op jit(solution)/shard_map/all_to_all | solution.py:40
  71.7 60.9 %all-to-all-start.1 = ((bf16[32,40,896]{2,1,0:T(8,128)(2,1)}), bf16[32,40,896]{2,1,0:T(8,128)(2,1)}, u32[]{:S(2)}, u32[]{:S(2)}) async-start(bf16[32,40,896]{2,1,0:T(8,128)(2,1)} %bitcast.37), calls=%async_computation.1 | async-start | bytes 4587520 | tf_op jit(solution)/shard_map/all_to_all | solution.py:40
  88.2 15.6 %copy-start.2 = (f32[4,160,1024]{2,1,0:T(8,128)S(1)}, f32[4,160,1024]{2,1,0:T(8,128)}, u32[]{:S(2)}) copy-start(f32[4,160,1024]{2,1,0:T(8,128)} %get-tuple-element.28) | copy-start | bytes 7864324
  88.3 3.3 %collective-permute-start = (bf16[4,160,1024]{2,1,0:T(8,128)(2,1)}, bf16[4,160,1024]{2,1,0:T(8,128)(2,1)S(1)}, u32[]{:S(2)}, u32[]{:S(2)}) collective-permute-start(bf16[4,160,1024]{2,1,0:T(8,128)(2,1)} %get-tuple-element.29), channel_id=1, source_target_pairs={{0,32},{32,0},{1,33},{33,1},{2,34},{34,2},{3,35},{35,3},{4,36},{36... | collective-permute-start | bytes 3932168 | tf_op jit(solution)/shard_map/ppermute | solution.py:31
  93.1 10.7 %collective-permute-start.1 = (bf16[2,160,1024]{2,1,0:T(8,128)(2,1)S(1)}, bf16[2,160,1024]{2,1,0:T(8,128)(2,1)S(1)}, u32[]{:S(2)}, u32[]{:S(2)}) collective-permute-start(bf16[2,160,1024]{2,1,0:T(8,128)(2,1)S(1)} %add_convert_fusion.1), channel_id=1, source_target_pairs={{0,64},{64,0},{128,192},{192,128},{32,224},{96,160},{160,96},{224,... | collective-permute-start | bytes 1966088 | tf_op jit(solution)/shard_map/ppermute | solution.py:27
  103.9 8.4 %collective-permute-start.2 = (bf16[160,1024]{1,0:T(8,128)(2,1)S(1)}, bf16[160,1024]{1,0:T(8,128)(2,1)S(1)}, u32[]{:S(2)}, u32[]{:S(2)}) collective-permute-start(bf16[160,1024]{1,0:T(8,128)(2,1)S(1)} %fusion), channel_id=1, source_target_pairs={{0,192},{64,128},{128,64},{192,0},{32,96},{96,32},{160,224},{224,1... | collective-permute-start | bytes 983048 | tf_op jit(solution)/shard_map/ppermute | solution.py:27
  113.4 7.1 %collective-permute-start.3 = (bf16[160,1024]{1,0:T(8,128)(2,1)S(1)}, bf16[160,1024]{1,0:T(8,128)(2,1)S(1)}, u32[]{:S(2)}, u32[]{:S(2)}) collective-permute-start(bf16[160,1024]{1,0:T(8,128)(2,1)S(1)} %get-tuple-element.45), channel_id=1, source_target_pairs={{0,64},{64,0},{128,192},{192,128},{32,224},{96,160},{160,96},{224,... | collective-permute-start | bytes 983048 | tf_op jit(solution)/shard_map/ppermute | solution.py:27
  120.6 23.6 %copy-start.5 = (bf16[2,160,1024]{2,1,0:T(8,128)(2,1)}, bf16[2,160,1024]{2,1,0:T(8,128)(2,1)S(1)}, u32[]{:S(2)}) copy-start(bf16[2,160,1024]{2,1,0:T(8,128)(2,1)S(1)} %pad_maximum_fusion.refs_0_) | copy-start | bytes 1966084
  120.6 12.0 %collective-permute-start.4 = (bf16[2,160,1024]{2,1,0:T(8,128)(2,1)S(1)}, bf16[2,160,1024]{2,1,0:T(8,128)(2,1)}, u32[]{:S(2)}, u32[]{:S(2)}) collective-permute-start(bf16[2,160,1024]{2,1,0:T(8,128)(2,1)S(1)} %pad_maximum_fusion.refs_0_), channel_id=1, source_target_pairs={{0,192},{64,128},{128,64},{192,0},{32,96},{96,32},{160,224},{224,1... | collective-permute-start | bytes 1966088 | tf_op jit(solution)/shard_map/ppermute | solution.py:27
  144.1 12.6 %collective-permute-start.7 = (bf16[4,160,1024]{2,1,0:T(8,128)(2,1)}, bf16[4,160,1024]{2,1,0:T(8,128)(2,1)}, u32[]{:S(2)}, u32[]{:S(2)}) collective-permute-start(bf16[4,160,1024]{2,1,0:T(8,128)(2,1)} %get-tuple-element.36), channel_id=1, source_target_pairs={{0,32},{32,0},{1,33},{33,1},{2,34},{34,2},{3,35},{35,3},{4,36},{36... | collective-permute-start | bytes 3932168 | tf_op jit(solution)/shard_map/ppermute | solution.py:31
  144.2 4.2 %collective-permute-start.5 = (bf16[2,160,1024]{2,1,0:T(8,128)(2,1)S(1)}, bf16[2,160,1024]{2,1,0:T(8,128)(2,1)S(1)}, u32[]{:S(2)}, u32[]{:S(2)}) collective-permute-start(bf16[2,160,1024]{2,1,0:T(8,128)(2,1)S(1)} %pad_maximum_fusion.refs_0_), channel_id=1, source_target_pairs={{0,32},{32,0},{1,33},{33,1},{2,34},{34,2},{3,35},{35,3},{4,36},{36... | collective-permute-start | bytes 1966088 | tf_op jit(solution)/shard_map/ppermute | solution.py:31
  144.7 4.7 %collective-permute-start.6 = (bf16[2,160,1024]{2,1,0:T(8,128)(2,1)}, bf16[2,160,1024]{2,1,0:T(8,128)(2,1)}, u32[]{:S(2)}, u32[]{:S(2)}) collective-permute-start(bf16[2,160,1024]{2,1,0:T(8,128)(2,1)} %collective-permute-done.4.refs_1_), channel_id=1, source_target_pairs={{0,32},{32,0},{1,33},{33,1},{2,34},{34,2},{3,35},{35,3},{4,36},{36... | collective-permute-start | bytes 1966088 | tf_op jit(solution)/shard_map/ppermute | solution.py:31
  158.8 64.3 %all-to-all-start.2 = ((bf16[32,40,896]{2,1,0:T(8,128)(2,1)}), bf16[32,40,896]{2,1,0:T(8,128)(2,1)S(1)}, u32[]{:S(2)}, u32[]{:S(2)}) async-start(bf16[32,40,896]{2,1,0:T(8,128)(2,1)} %bitcast.41), calls=%async_computation.2 | async-start | bytes 4587520 | tf_op jit(solution)/shard_map/all_to_all | solution.py:40
  168.5 10.9 %collective-permute-start.8 = (bf16[2,160,1024]{2,1,0:T(8,128)(2,1)}, bf16[2,160,1024]{2,1,0:T(8,128)(2,1)S(1)}, u32[]{:S(2)}, u32[]{:S(2)}) collective-permute-start(bf16[2,160,1024]{2,1,0:T(8,128)(2,1)} %add_convert_fusion), channel_id=1, source_target_pairs={{0,64},{64,0},{128,192},{192,128},{32,224},{96,160},{160,96},{224,... | collective-permute-start | bytes 1966088 | tf_op jit(solution)/shard_map/ppermute | solution.py:27
  181.0 8.4 %collective-permute-start.9 = (bf16[160,1024]{1,0:T(8,128)(2,1)S(1)}, bf16[160,1024]{1,0:T(8,128)(2,1)S(1)}, u32[]{:S(2)}, u32[]{:S(2)}) collective-permute-start(bf16[160,1024]{1,0:T(8,128)(2,1)S(1)} %fusion.1), channel_id=1, source_target_pairs={{0,192},{64,128},{128,64},{192,0},{32,96},{96,32},{160,224},{224,1... | collective-permute-start | bytes 983048 | tf_op jit(solution)/shard_map/ppermute | solution.py:27
  192.8 7.3 %collective-permute-start.10 = (bf16[160,1024]{1,0:T(8,128)(2,1)}, bf16[160,1024]{1,0:T(8,128)(2,1)S(1)}, u32[]{:S(2)}, u32[]{:S(2)}) collective-permute-start(bf16[160,1024]{1,0:T(8,128)(2,1)} %grad_share.1), channel_id=1, source_target_pairs={{0,64},{64,0},{128,192},{192,128},{32,224},{96,160},{160,96},{224,... | collective-permute-start | bytes 983048 | tf_op jit(solution)/shard_map/ppermute | solution.py:27
  201.2 14.3 %copy-start.6 = (bf16[2,160,1024]{2,1,0:T(8,128)(2,1)}, bf16[2,160,1024]{2,1,0:T(8,128)(2,1)S(1)}, u32[]{:S(2)}) copy-start(bf16[2,160,1024]{2,1,0:T(8,128)(2,1)S(1)} %pad_maximum_fusion.1.refs_0_) | copy-start | bytes 1966084
  201.2 12.1 %collective-permute-start.11 = (bf16[2,160,1024]{2,1,0:T(8,128)(2,1)S(1)}, bf16[2,160,1024]{2,1,0:T(8,128)(2,1)S(1)}, u32[]{:S(2)}, u32[]{:S(2)}) collective-permute-start(bf16[2,160,1024]{2,1,0:T(8,128)(2,1)S(1)} %pad_maximum_fusion.1.refs_0_), channel_id=1, source_target_pairs={{0,192},{64,128},{128,64},{192,0},{32,96},{96,32},{160,224},{224,1... | collective-permute-start | bytes 1966088 | tf_op jit(solution)/shard_map/ppermute | solution.py:27
  201.7 11.6 %collective-permute-start.12 = (bf16[2,160,1024]{2,1,0:T(8,128)(2,1)S(1)}, bf16[2,160,1024]{2,1,0:T(8,128)(2,1)S(1)}, u32[]{:S(2)}, u32[]{:S(2)}) collective-permute-start(bf16[2,160,1024]{2,1,0:T(8,128)(2,1)S(1)} %pad_maximum_fusion.1.refs_0_), channel_id=1, source_target_pairs={{0,32},{32,0},{1,33},{33,1},{2,34},{34,2},{3,35},{35,3},{4,36},{36... | collective-permute-start | bytes 1966088 | tf_op jit(solution)/shard_map/ppermute | solution.py:31
  213.2 2.2 collective-permute-start.13
  224.5 64.2 %all-to-all-start.3 = ((bf16[32,40,896]{2,1,0:T(8,128)(2,1)}), bf16[32,40,896]{2,1,0:T(8,128)(2,1)}, u32[]{:S(2)}, u32[]{:S(2)}) async-start(bf16[32,40,896]{2,1,0:T(8,128)(2,1)} %bitcast.42), calls=%async_computation.3 | async-start | bytes 4587520 | tf_op jit(solution)/shard_map/all_to_all | solution.py:40
  238.4 8.0 %collective-permute-start.14 = (f32[32,128]{1,0:T(8,128)}, f32[32,128]{1,0:T(8,128)S(1)}, u32[]{:S(2)}, u32[]{:S(2)}) collective-permute-start(f32[32,128]{1,0:T(8,128)} %gate_terms.1), channel_id=1, source_target_pairs={{0,32},{32,0},{1,33},{33,1},{2,34},{34,2},{3,35},{35,3},{4,36},{36... | collective-permute-start | bytes 49160 | tf_op jit(solution)/shard_map/ppermute | solution.py:31
  246.5 6.7 %collective-permute-start.15 = (f32[32,128]{1,0:T(8,128)S(1)}, f32[32,128]{1,0:T(8,128)S(1)}, u32[]{:S(2)}, u32[]{:S(2)}) collective-permute-start(f32[32,128]{1,0:T(8,128)S(1)} %add.102), channel_id=1, source_target_pairs={{0,64},{64,0},{128,192},{192,128},{32,96},{96,32},{160,224},{224,1... | collective-permute-start | bytes 49160 | tf_op jit(solution)/shard_map/ppermute | solution.py:27
  253.2 5.0 %collective-permute-start.16 = (f32[32,128]{1,0:T(8,128)S(1)}, f32[32,128]{1,0:T(8,128)S(1)}, u32[]{:S(2)}, u32[]{:S(2)}) collective-permute-start(f32[32,128]{1,0:T(8,128)S(1)} %add.103), channel_id=1, source_target_pairs={{0,192},{64,128},{128,64},{192,0},{32,224},{96,160},{160,96},{224,... | collective-permute-start | bytes 49160 | tf_op jit(solution)/shard_map/ppermute | solution.py:27
  (10 other events, 41.0 us)
where the time goes:
time: 294 us; the launch traced here: 293 us
  waiting for transfers between devices  161 us (55%)
  Pallas kernels  75.8 us (26%)
  starting transfers between devices  39.8 us (14%)
  other arithmetic  8.25 us (3%)
  local copies, waits for them, and re-layouts  6.71 us (2%)
    all_to_all x4, waiting for transfers between devices, scatter(): lax.all_to_all(parts, ('z', 'x'), split_axis=0, concat_axis=0, tiled=True)  79.3 us
    ppermute x10, waiting for transfers between devices, swap(): return lax.ppermute(value, ('y', 'core'), pairs)  74.5 us
    all_to_all x4, starting transfers between devices, scatter(): lax.all_to_all(parts, ('z', 'x'), split_axis=0, concat_axis=0, tiled=True)  36.2 us
    pallas_call x2, Pallas kernels, partial_sums(): pl.pallas_call(kernel, grid=(hid // step,), out_shape=[jax.ShapeDtypeStru...  22.5 us
    pallas_call x2, Pallas kernels, weight_grads(): pl.pallas_call(kernel, grid=(count // step,), out_shape=jax.ShapeDtypeStr...  14.6 us
    pallas_call x2, Pallas kernels, expand_rows(): pl.pallas_call(kernel, out_shape=[jax.ShapeDtypeStruct((NY, 2 * rows, wid...  14.6 us
    pallas_call x2, Pallas kernels, mix_rows(): pl.pallas_call(kernel, grid=(CHUNKS,), out_shape=jax.ShapeDtypeStruct((to...  8.62 us
    ppermute x7, waiting for transfers between devices, swap_core(): return lax.ppermute(value, 'core', [(0, 1), (1, 0)])  7.53 us
  transfers between devices with their start and end apart: 21, of which 16 were waited for; matrix products, arithmetic and copies ran while one was open for 2% of the time, Pallas kernels for 19%

commit v1 on v0

--- a/solution.py
+++ b/solution.py
@@ -68,18 +68,17 @@
 
 
 def mix_rows(picks, rows):
-    slots, tok = picks[0].shape
+    tok, slots = picks[0].shape
     width = rows.shape[1]
-    step = slots // CHUNKS
+    count = 2
+    step = slots // count
 
     def kernel(*refs):
         pick_refs, (rows_ref, out, total) = refs[: len(picks)], refs[len(picks) :]
         k = pl.program_id(0)
         part = None
         for ref in pick_refs:
-            more = lax.dot_general(
-                ref[...], rows_ref[...], (((0,), (0,)), ((), ())), preferred_element_type=F32
-            )
+            more = jnp.dot(ref[...], rows_ref[...], preferred_element_type=F32)
             part = more if part is None else part + more
 
         @pl.when(k == 0)
@@ -90,15 +89,15 @@
         def _():
             total[...] += part
 
-        @pl.when(k == CHUNKS - 1)
+        @pl.when(k == count - 1)
         def _():
             out[...] = total[...].astype(BF)
 
     return pl.pallas_call(
         kernel,
-        grid=(CHUNKS,),
+        grid=(count,),
         out_shape=jax.ShapeDtypeStruct((tok, width), BF),
-        in_specs=[pl.BlockSpec((step, tok), lambda k: (k, 0))] * len(picks)
+        in_specs=[pl.BlockSpec((tok, step), lambda k: (0, k))] * len(picks)
         + [pl.BlockSpec((step, width), lambda k: (k, 0))],
         out_specs=pl.BlockSpec((tok, width), lambda k: (0, 0)),
         scratch_shapes=[pltpu.VMEM((tok, width), F32)],
@@ -149,34 +148,29 @@
     step = 256
 
     def kernel(table_ref, weight_ref, rows_ref, keep, away, held, sems):
-        first = pl.program_id(0) == 0
-        core = table_ref[4 * NY]
-
-        def get(i, h):
-            return pltpu.make_async_copy(
-                rows_ref.at[i, h ^ core], held.at[pl.ds((2 * i + h) * rows, rows)], sems.at[i, h]
-            )
-
-        @pl.when(first)
+        @pl.when(pl.program_id(0) == 0)
         def _():
-            for i in range(NY):
-                for h in range(2):
-                    get(i, h).start()
-
+            core = table_ref[4 * NY]
+            copies = [
+                pltpu.make_async_copy(
+                    rows_ref.at[i, h ^ core], held.at[pl.ds((2 * i + h) * rows, rows)], sems.at[i, h]
+                )
+                for i in range(NY)
+                for h in range(2)
+            ]
+            for c in copies:
+                c.start()
+            for c in copies:
+                c.wait()
+
+        made = lax.dot_general(
+            held[...], weight_ref[...], (((1,), (contract,)), ((), ())),
+            preferred_element_type=F32,
+        )
         for i in range(NY):
             at = i * 2 * rows
-
-            @pl.when(first)
-            def _():
-                for h in range(2):
-                    get(i, h).wait()
-
-            made = lax.dot_general(
-                held[at : at + 2 * rows], weight_ref[...], (((1,), (contract,)), ((), ())),
-                preferred_element_type=F32,
-            )
-            keep[table_ref[i]] = made[:rows]
-            away[table_ref[NY + i]] = made[rows:].astype(BF)
+            keep[table_ref[i]] = made[at : at + rows]
+            away[table_ref[NY + i]] = made[at + rows : at + 2 * rows].astype(BF)
 
     if contract == 0:
         weight_spec = pl.BlockSpec((width, step), lambda n: (0, n))
@@ -424,7 +418,7 @@
     dx_rows, pre_grad = expand_rows(table, grads, w_up, 1)
     dx_back = scatter(tie(dx_rows, out_back))
 
-    mixed = mix_rows((gate_hi, gate_lo), out_back)
+    mixed = mix_rows((gate_hi.T, gate_lo.T), out_back)
     terms = gate_terms(pick, tie(out_back, dx_rows), cotangent)
     terms = terms + swap_core(terms)
     terms = terms + swap(terms, 0, False)
@@ -433,7 +427,7 @@
     gate_grads = jnp.sum(jnp.where(own, terms[None], 0.0), axis=1).T
     down_grad = weight_grads(tie(hidden, dx_rows), g_slots, 256)
     up_grad = weight_grads(x_slots, pre_grad, 128)
-    input_grads = mix_rows((pick,), tie(dx_back, down_grad, up_grad, mixed))
+    input_grads = mix_rows((pick.T,), tie(dx_back, down_grad, up_grad, mixed))
     return mixed, input_grads, up_grad[None], down_grad[None], gate_grads
 
 

time: 294 us -> 286 us (0.973)
  Pallas kernels: 75.8 us -> 66.3 us
    pallas_call x2, Pallas kernels: 22.5 us -> 15.3 us  [partial_sums(): pl.pallas_call(kernel, grid=(hid // step,), out_shape=[jax.ShapeDtypeStru...]
    unnamed x26 -> x32, local copies, waits for them, and re-layouts: 6.11 us -> 6.13 us
  transfers between devices with their start and end apart: 21 -> 21, of which waited for: 16 -> 17; matrix products, arithmetic and copies ran while one was open for 2% -> 3% of each run, Pallas kernels for 19% -> 18%
where the time goes in v1:
time: 286 us; the launch traced here: 284 us
  waiting for transfers between devices  162 us (57%)
  Pallas kernels  66.3 us (23%)
  starting transfers between devices  37.4 us (13%)
  local copies, waits for them, and re-layouts  9.48 us (3%)
  other arithmetic  8.25 us (3%)
    all_to_all x4, waiting for transfers between devices, scatter(): lax.all_to_all(parts, ('z', 'x'), split_axis=0, concat_axis=0, tiled=True)  78.8 us
    ppermute x10, waiting for transfers between devices, swap(): return lax.ppermute(value, ('y', 'core'), pairs)  75.6 us
    all_to_all x4, starting transfers between devices, scatter(): lax.all_to_all(parts, ('z', 'x'), split_axis=0, concat_axis=0, tiled=True)  34 us
    pallas_call x2, Pallas kernels, partial_sums(): pl.pallas_call(kernel, grid=(hid // step,), out_shape=[jax.ShapeDtypeStru...  15.3 us
    pallas_call x2, Pallas kernels, weight_grads(): pl.pallas_call(kernel, grid=(count // step,), out_shape=jax.ShapeDtypeStr...  14.7 us
    pallas_call x2, Pallas kernels, expand_rows(): pl.pallas_call(kernel, out_shape=[jax.ShapeDtypeStruct((NY, 2 * rows, wid...  14.6 us
    ppermute x7, waiting for transfers between devices, swap_core(): return lax.ppermute(value, 'core', [(0, 1), (1, 0)])  7.52 us
    pallas_call x2, Pallas kernels, mix_rows(): pl.pallas_call(kernel, grid=(count,), out_shape=jax.ShapeDtypeStruct((tok...  6.26 us
  transfers between devices with their start and end apart: 21, of which 17 were waited for; matrix products, arithmetic and copies ran while one was open for 3% of the time, Pallas kernels for 18%

profile of v1, /device:TPU:24, one launch (start us, length us, event | category | flops | bytes accessed | tf_op | source)
XLA Modules:
  0.0 284.3 jit_solution(3629472618579265748)
XLA Ops:
  0.6 4.0 %route.1 = (bf16[1280,128]{1,0:T(8,128)(2,1)}, bf16[1280,128]{1,0:T(8,128)(2,1)}, bf16[1280,128]{1,0:T(8,128)(2,1)}, bf16[1280,896]{1,0:T(8,128)(2,1)}) custom-call(s32[8,128]{1,0:T(8,128)} %bitcast.53, f32[8,128]{1,0:T(8,128)} %bitcast.56, bf16[128,896]{1,0:T(8,128)(2,1)} %tokens_ref.1), custom_call_target="tpu_custom_call" | custom-call | tf_op jit(solution)/shard_map/route/pallas_call | solution.py:379
  4.6 11.3 %all-to-all-start = ((bf16[32,40,896]{2,1,0:T(8,128)(2,1)}), bf16[32,40,896]{2,1,0:T(8,128)(2,1)S(1)}, u32[]{:S(2)}, u32[]{:S(2)}) async-start(bf16[32,40,896]{2,1,0:T(8,128)(2,1)} %bitcast.43), calls=%async_computation | async-start | bytes 4587520 | tf_op jit(solution)/shard_map/all_to_all | solution.py:40
  16.7 4.4 %select_scaled.1 = bf16[1280,896]{1,0:T(8,128)(2,1)} custom-call(bf16[1280,128]{1,0:T(8,128)(2,1)} %get-tuple-element.30.pick_ref, bf16[1280,128]{1,0:T(8,128)(2,1)} %get-tuple-element.25.refs_0_, bf16[1280,128]{1,0:T(8,128)(2,1)} %get-tuple-element.26.refs_1_, bf16[128,896]{1,0:T(8,128)(2,1)} %values_ref.1), custom_call_target="tpu_custom_call" | custom-call | flops 300000000 | bytes 3000000 | tf_op jit(solution)/shard_map/select_scaled/pallas_call | solution.py:59
  21.1 49.2 %all-to-all-done = bf16[32,40,896]{2,1,0:T(8,128)(2,1)S(1)} async-done(((bf16[32,40,896]{2,1,0:T(8,128)(2,1)}), bf16[32,40,896]{2,1,0:T(8,128)(2,1)S(1)}, u32[]{:S(2)}, u32[]{:S(2)}) %all-to-all-start) | async-done | bytes 2293792 | tf_op jit(solution)/shard_map/all_to_all | solution.py:40
  71.7 5.5 %all-to-all-start.1 = ((bf16[32,40,896]{2,1,0:T(8,128)(2,1)}), bf16[32,40,896]{2,1,0:T(8,128)(2,1)}, u32[]{:S(2)}, u32[]{:S(2)}) async-start(bf16[32,40,896]{2,1,0:T(8,128)(2,1)} %bitcast.40), calls=%async_computation.1 | async-start | bytes 4587520 | tf_op jit(solution)/shard_map/all_to_all | solution.py:40
  77.2 7.6 %shard_map.101 = (f32[4,160,1024]{2,1,0:T(8,128)}, bf16[4,160,1024]{2,1,0:T(8,128)(2,1)}) custom-call(s32[17]{0:T(128)} %concatenate.3.table_ref, bf16[896,1024]{1,0:T(8,128)(2,1)} %bitcast.59, bf16[4,2,160,896]{3,2,1,0:T(8,128)(2,1)} %bitcast.41), custom_call_target="tpu_custom_call" | custom-call | flops 2400000000 | bytes 9000000 | tf_op jit(solution)/shard_map/pallas_call | solution.py:180
  90.6 9.8 %collective-permute-done.1 = bf16[2,160,1024]{2,1,0:T(8,128)(2,1)S(1)} collective-permute-done((bf16[2,160,1024]{2,1,0:T(8,128)(2,1)S(1)}, bf16[2,160,1024]{2,1,0:T(8,128)(2,1)S(1)}, u32[]{:S(2)}, u32[]{:S(2)}) %collective-permute-start.1) | collective-permute-done | bytes 655392 | tf_op jit(solution)/shard_map/ppermute | solution.py:27
  100.9 8.1 %collective-permute-done.2 = bf16[160,1024]{1,0:T(8,128)(2,1)S(1)} collective-permute-done((bf16[160,1024]{1,0:T(8,128)(2,1)S(1)}, bf16[160,1024]{1,0:T(8,128)(2,1)S(1)}, u32[]{:S(2)}, u32[]{:S(2)}) %collective-permute-start.2) | collective-permute-done | bytes 327712 | tf_op jit(solution)/shard_map/ppermute | solution.py:27
  110.0 7.1 %collective-permute-done.3 = bf16[160,1024]{1,0:T(8,128)(2,1)S(1)} collective-permute-done((bf16[160,1024]{1,0:T(8,128)(2,1)S(1)}, bf16[160,1024]{1,0:T(8,128)(2,1)S(1)}, u32[]{:S(2)}, u32[]{:S(2)}) %collective-permute-start.3) | collective-permute-done | bytes 327712 | tf_op jit(solution)/shard_map/ppermute | solution.py:27
  117.5 11.7 %collective-permute-done.4.refs_1_ = bf16[2,160,1024]{2,1,0:T(8,128)(2,1)} collective-permute-done((bf16[2,160,1024]{2,1,0:T(8,128)(2,1)S(1)}, bf16[2,160,1024]{2,1,0:T(8,128)(2,1)}, u32[]{:S(2)}, u32[]{:S(2)}) %collective-permute-start.4) | collective-permute-done | bytes 655392 | tf_op jit(solution)/shard_map/ppermute | solution.py:27
  131.2 7.7 %shard_map.102 = (f32[4,160,1024]{2,1,0:T(8,128)}, bf16[4,160,1024]{2,1,0:T(8,128)(2,1)}) custom-call(s32[17]{0:T(128)} %concatenate.3.table_ref, bf16[1024,896]{1,0:T(8,128)(2,1)} %bitcast.57, bf16[4,2,160,896]{3,2,1,0:T(8,128)(2,1)} %bitcast.18.rows_ref), custom_call_target="tpu_custom_call" | custom-call | flops 2400000000 | bytes 9000000 | tf_op jit(solution)/shard_map/pallas_call | solution.py:180
  139.6 3.6 %collective-permute-done.5.refs_2_ = bf16[2,160,1024]{2,1,0:T(8,128)(2,1)S(1)} collective-permute-done((bf16[2,160,1024]{2,1,0:T(8,128)(2,1)S(1)}, bf16[2,160,1024]{2,1,0:T(8,128)(2,1)S(1)}, u32[]{:S(2)}, u32[]{:S(2)}) %collective-permute-start.5) | collective-permute-done | bytes 655392 | tf_op jit(solution)/shard_map/ppermute | solution.py:31
  144.3 7.2 %shard_map.103 = (bf16[4,320,896]{2,1,0:T(8,128)(2,1)}, bf16[4,2,160,1024]{3,2,1,0:T(8,128)(2,1)}) custom-call(s32[17]{0:T(128)} %concatenate.3.table_ref, bf16[1024,896]{1,0:T(8,128)(2,1)} %bitcast.58, bf16[2,160,1024]{2,1,0:T(8,128)(2,1)} %copy-done.8, bf16[2,160,1024]{2,1,0:T(8,128)(2,1)} %collective-permute-done.4.refs_1_, ...), custom_call_target="tpu_custom_call" | custom-call | flops 2400000000 | bytes 9000000 | tf_op jit(solution)/shard_map/pallas_call | solution.py:238
  153.7 7.7 %all-to-all-start.2 = ((bf16[32,40,896]{2,1,0:T(8,128)(2,1)}), bf16[32,40,896]{2,1,0:T(8,128)(2,1)S(1)}, u32[]{:S(2)}, u32[]{:S(2)}) async-start(bf16[32,40,896]{2,1,0:T(8,128)(2,1)} %bitcast.44), calls=%async_computation.2 | async-start | bytes 4587520 | tf_op jit(solution)/shard_map/all_to_all | solution.py:40
  161.4 10.8 %collective-permute-done.8.near_ref = bf16[2,160,1024]{2,1,0:T(8,128)(2,1)S(1)} collective-permute-done((bf16[2,160,1024]{2,1,0:T(8,128)(2,1)}, bf16[2,160,1024]{2,1,0:T(8,128)(2,1)S(1)}, u32[]{:S(2)}, u32[]{:S(2)}) %collective-permute-start.8) | collective-permute-done | bytes 655392 | tf_op jit(solution)/shard_map/ppermute | solution.py:27
  174.1 8.1 %collective-permute-done.9.last_ref = bf16[160,1024]{1,0:T(8,128)(2,1)S(1)} collective-permute-done((bf16[160,1024]{1,0:T(8,128)(2,1)S(1)}, bf16[160,1024]{1,0:T(8,128)(2,1)S(1)}, u32[]{:S(2)}, u32[]{:S(2)}) %collective-permute-start.9) | collective-permute-done | bytes 327712 | tf_op jit(solution)/shard_map/ppermute | solution.py:27
  185.7 7.3 %collective-permute-done.10 = bf16[160,1024]{1,0:T(8,128)(2,1)S(1)} collective-permute-done((bf16[160,1024]{1,0:T(8,128)(2,1)}, bf16[160,1024]{1,0:T(8,128)(2,1)S(1)}, u32[]{:S(2)}, u32[]{:S(2)}) %collective-permute-start.10) | collective-permute-done | bytes 327712 | tf_op jit(solution)/shard_map/ppermute | solution.py:27
  194.4 11.5 %collective-permute-done.11.refs_1_ = bf16[2,160,1024]{2,1,0:T(8,128)(2,1)S(1)} collective-permute-done((bf16[2,160,1024]{2,1,0:T(8,128)(2,1)S(1)}, bf16[2,160,1024]{2,1,0:T(8,128)(2,1)S(1)}, u32[]{:S(2)}, u32[]{:S(2)}) %collective-permute-start.11) | collective-permute-done | bytes 655392 | tf_op jit(solution)/shard_map/ppermute | solution.py:27
  208.1 7.4 %shard_map.105 = (bf16[4,320,896]{2,1,0:T(8,128)(2,1)}, bf16[4,2,160,1024]{3,2,1,0:T(8,128)(2,1)}) custom-call(s32[17]{0:T(128)} %concatenate.3.table_ref, bf16[896,1024]{1,0:T(8,128)(2,1)} %bitcast.60, bf16[2,160,1024]{2,1,0:T(8,128)(2,1)} %copy-done.9, bf16[2,160,1024]{2,1,0:T(8,128)(2,1)} %copy-done.13, bf16[2,160,1024]{2,1,0:T(8,128)(2,1)} %copy-done.14, ...), custom_call_target="tpu_custom_call" | custom-call | flops 2400000000 | bytes 9000000 | tf_op jit(solution)/shard_map/pallas_call | solution.py:238
  217.3 9.5 %all-to-all-start.3 = ((bf16[32,40,896]{2,1,0:T(8,128)(2,1)}), bf16[32,40,896]{2,1,0:T(8,128)(2,1)}, u32[]{:S(2)}, u32[]{:S(2)}) async-start(bf16[32,40,896]{2,1,0:T(8,128)(2,1)} %bitcast.45), calls=%async_computation.3 | async-start | bytes 4587520 | tf_op jit(solution)/shard_map/all_to_all | solution.py:40
  229.6 4.3 %gate_terms.1 = f32[32,128]{1,0:T(8,128)} custom-call(bf16[1280,128]{1,0:T(8,128)(2,1)} %get-tuple-element.30.pick_ref, bf16[1280,896]{1,0:T(8,128)(2,1)} %bitcast.38, bf16[128,896]{1,0:T(8,128)(2,1)} %values_ref.1), custom_call_target="tpu_custom_call" | custom-call | flops 300000000 | bytes 3000000 | tf_op jit(solution)/shard_map/gate_terms/pallas_call | solution.py:129
  233.8 8.0 %shard_map.107 = bf16[896,1024]{1,0:T(8,128)(2,1)} custom-call(bf16[1280,896]{1,0:T(8,128)(2,1)} %bitcast.42, bf16[1280,1024]{1,0:T(8,128)(2,1)} %bitcast.62), custom_call_target="tpu_custom_call" | custom-call | flops 2400000000 | bytes 7000000 | tf_op jit(solution)/shard_map/pallas_call | solution.py:271
  242.0 6.6 %shard_map.106 = bf16[1024,896]{1,0:T(8,128)(2,1)} custom-call(bf16[1280,1024]{1,0:T(8,128)(2,1)} %bitcast.61, bf16[1280,896]{1,0:T(8,128)(2,1)} %bitcast.17.right_ref), custom_call_target="tpu_custom_call" | custom-call | flops 2400000000 | bytes 7000000 | tf_op jit(solution)/shard_map/pallas_call | solution.py:271
  254.3 27.1 %all-to-all-done.3 = bf16[32,40,896]{2,1,0:T(8,128)(2,1)} async-done(((bf16[32,40,896]{2,1,0:T(8,128)(2,1)}), bf16[32,40,896]{2,1,0:T(8,128)(2,1)}, u32[]{:S(2)}, u32[]{:S(2)}) %all-to-all-start.3) | async-done | bytes 2293792 | tf_op jit(solution)/shard_map/all_to_all | solution.py:40
  (79 shorter events, 38.0 us)
Async XLA Ops:
  4.6 65.6 %all-to-all-start = ((bf16[32,40,896]{2,1,0:T(8,128)(2,1)}), bf16[32,40,896]{2,1,0:T(8,128)(2,1)S(1)}, u32[]{:S(2)}, u32[]{:S(2)}) async-start(bf16[32,40,896]{2,1,0:T(8,128)(2,1)} %bitcast.43), calls=%async_computation | async-start | bytes 4587520 | tf_op jit(solution)/shard_map/all_to_all | solution.py:40
  71.7 59.5 %all-to-all-start.1 = ((bf16[32,40,896]{2,1,0:T(8,128)(2,1)}), bf16[32,40,896]{2,1,0:T(8,128)(2,1)}, u32[]{:S(2)}, u32[]{:S(2)}) async-start(bf16[32,40,896]{2,1,0:T(8,128)(2,1)} %bitcast.40), calls=%async_computation.1 | async-start | bytes 4587520 | tf_op jit(solution)/shard_map/all_to_all | solution.py:40
  84.9 15.6 %copy-start.3 = (f32[4,160,1024]{2,1,0:T(8,128)S(1)}, f32[4,160,1024]{2,1,0:T(8,128)}, u32[]{:S(2)}) copy-start(f32[4,160,1024]{2,1,0:T(8,128)} %get-tuple-element.28) | copy-start | bytes 7864324
  84.9 3.3 %collective-permute-start = (bf16[4,160,1024]{2,1,0:T(8,128)(2,1)}, bf16[4,160,1024]{2,1,0:T(8,128)(2,1)S(1)}, u32[]{:S(2)}, u32[]{:S(2)}) collective-permute-start(bf16[4,160,1024]{2,1,0:T(8,128)(2,1)} %get-tuple-element.29), channel_id=1, source_target_pairs={{0,32},{32,0},{1,33},{33,1},{2,34},{34,2},{3,35},{35,3},{4,36},{36... | collective-permute-start | bytes 3932168 | tf_op jit(solution)/shard_map/ppermute | solution.py:31
  89.7 10.7 %collective-permute-start.1 = (bf16[2,160,1024]{2,1,0:T(8,128)(2,1)S(1)}, bf16[2,160,1024]{2,1,0:T(8,128)(2,1)S(1)}, u32[]{:S(2)}, u32[]{:S(2)}) collective-permute-start(bf16[2,160,1024]{2,1,0:T(8,128)(2,1)S(1)} %add_convert_fusion.1), channel_id=1, source_target_pairs={{0,64},{64,0},{128,192},{192,128},{32,224},{96,160},{160,96},{224,... | collective-permute-start | bytes 1966088 | tf_op jit(solution)/shard_map/ppermute | solution.py:27
  100.6 8.4 %collective-permute-start.2 = (bf16[160,1024]{1,0:T(8,128)(2,1)S(1)}, bf16[160,1024]{1,0:T(8,128)(2,1)S(1)}, u32[]{:S(2)}, u32[]{:S(2)}) collective-permute-start(bf16[160,1024]{1,0:T(8,128)(2,1)S(1)} %fusion), channel_id=1, source_target_pairs={{0,192},{64,128},{128,64},{192,0},{32,96},{96,32},{160,224},{224,1... | collective-permute-start | bytes 983048 | tf_op jit(solution)/shard_map/ppermute | solution.py:27
  110.0 7.1 %collective-permute-start.3 = (bf16[160,1024]{1,0:T(8,128)(2,1)S(1)}, bf16[160,1024]{1,0:T(8,128)(2,1)S(1)}, u32[]{:S(2)}, u32[]{:S(2)}) collective-permute-start(bf16[160,1024]{1,0:T(8,128)(2,1)S(1)} %get-tuple-element.45), channel_id=1, source_target_pairs={{0,64},{64,0},{128,192},{192,128},{32,224},{96,160},{160,96},{224,... | collective-permute-start | bytes 983048 | tf_op jit(solution)/shard_map/ppermute | solution.py:27
  117.2 21.8 %copy-start.8 = (bf16[2,160,1024]{2,1,0:T(8,128)(2,1)}, bf16[2,160,1024]{2,1,0:T(8,128)(2,1)S(1)}, u32[]{:S(2)}) copy-start(bf16[2,160,1024]{2,1,0:T(8,128)(2,1)S(1)} %pad_maximum_fusion.refs_0_) | copy-start | bytes 1966084
  117.2 12.0 %collective-permute-start.4 = (bf16[2,160,1024]{2,1,0:T(8,128)(2,1)S(1)}, bf16[2,160,1024]{2,1,0:T(8,128)(2,1)}, u32[]{:S(2)}, u32[]{:S(2)}) collective-permute-start(bf16[2,160,1024]{2,1,0:T(8,128)(2,1)S(1)} %pad_maximum_fusion.refs_0_), channel_id=1, source_target_pairs={{0,192},{64,128},{128,64},{192,0},{32,96},{96,32},{160,224},{224,1... | collective-permute-start | bytes 1966088 | tf_op jit(solution)/shard_map/ppermute | solution.py:27
  138.9 12.6 %collective-permute-start.7 = (bf16[4,160,1024]{2,1,0:T(8,128)(2,1)}, bf16[4,160,1024]{2,1,0:T(8,128)(2,1)}, u32[]{:S(2)}, u32[]{:S(2)}) collective-permute-start(bf16[4,160,1024]{2,1,0:T(8,128)(2,1)} %get-tuple-element.36), channel_id=1, source_target_pairs={{0,32},{32,0},{1,33},{33,1},{2,34},{34,2},{3,35},{35,3},{4,36},{36... | collective-permute-start | bytes 3932168 | tf_op jit(solution)/shard_map/ppermute | solution.py:31
  139.0 4.2 %collective-permute-start.5 = (bf16[2,160,1024]{2,1,0:T(8,128)(2,1)S(1)}, bf16[2,160,1024]{2,1,0:T(8,128)(2,1)S(1)}, u32[]{:S(2)}, u32[]{:S(2)}) collective-permute-start(bf16[2,160,1024]{2,1,0:T(8,128)(2,1)S(1)} %pad_maximum_fusion.refs_0_), channel_id=1, source_target_pairs={{0,32},{32,0},{1,33},{33,1},{2,34},{34,2},{3,35},{35,3},{4,36},{36... | collective-permute-start | bytes 1966088 | tf_op jit(solution)/shard_map/ppermute | solution.py:31
  139.5 4.7 %collective-permute-start.6 = (bf16[2,160,1024]{2,1,0:T(8,128)(2,1)}, bf16[2,160,1024]{2,1,0:T(8,128)(2,1)}, u32[]{:S(2)}, u32[]{:S(2)}) collective-permute-start(bf16[2,160,1024]{2,1,0:T(8,128)(2,1)} %collective-permute-done.4.refs_1_), channel_id=1, source_target_pairs={{0,32},{32,0},{1,33},{33,1},{2,34},{34,2},{3,35},{35,3},{4,36},{36... | collective-permute-start | bytes 1966088 | tf_op jit(solution)/shard_map/ppermute | solution.py:31
  153.7 62.3 %all-to-all-start.2 = ((bf16[32,40,896]{2,1,0:T(8,128)(2,1)}), bf16[32,40,896]{2,1,0:T(8,128)(2,1)S(1)}, u32[]{:S(2)}, u32[]{:S(2)}) async-start(bf16[32,40,896]{2,1,0:T(8,128)(2,1)} %bitcast.44), calls=%async_computation.2 | async-start | bytes 4587520 | tf_op jit(solution)/shard_map/all_to_all | solution.py:40
  161.3 10.9 %collective-permute-start.8 = (bf16[2,160,1024]{2,1,0:T(8,128)(2,1)}, bf16[2,160,1024]{2,1,0:T(8,128)(2,1)S(1)}, u32[]{:S(2)}, u32[]{:S(2)}) collective-permute-start(bf16[2,160,1024]{2,1,0:T(8,128)(2,1)} %add_convert_fusion), channel_id=1, source_target_pairs={{0,64},{64,0},{128,192},{192,128},{32,224},{96,160},{160,96},{224,... | collective-permute-start | bytes 1966088 | tf_op jit(solution)/shard_map/ppermute | solution.py:27
  173.8 8.4 %collective-permute-start.9 = (bf16[160,1024]{1,0:T(8,128)(2,1)S(1)}, bf16[160,1024]{1,0:T(8,128)(2,1)S(1)}, u32[]{:S(2)}, u32[]{:S(2)}) collective-permute-start(bf16[160,1024]{1,0:T(8,128)(2,1)S(1)} %fusion.1), channel_id=1, source_target_pairs={{0,192},{64,128},{128,64},{192,0},{32,96},{96,32},{160,224},{224,1... | collective-permute-start | bytes 983048 | tf_op jit(solution)/shard_map/ppermute | solution.py:27
  185.7 7.3 %collective-permute-start.10 = (bf16[160,1024]{1,0:T(8,128)(2,1)}, bf16[160,1024]{1,0:T(8,128)(2,1)S(1)}, u32[]{:S(2)}, u32[]{:S(2)}) collective-permute-start(bf16[160,1024]{1,0:T(8,128)(2,1)} %grad_share.1), channel_id=1, source_target_pairs={{0,64},{64,0},{128,192},{192,128},{32,224},{96,160},{160,96},{224,... | collective-permute-start | bytes 983048 | tf_op jit(solution)/shard_map/ppermute | solution.py:27
  194.0 14.1 %copy-start.9 = (bf16[2,160,1024]{2,1,0:T(8,128)(2,1)}, bf16[2,160,1024]{2,1,0:T(8,128)(2,1)S(1)}, u32[]{:S(2)}) copy-start(bf16[2,160,1024]{2,1,0:T(8,128)(2,1)S(1)} %pad_maximum_fusion.1.refs_0_) | copy-start | bytes 1966084
  194.0 11.9 %collective-permute-start.11 = (bf16[2,160,1024]{2,1,0:T(8,128)(2,1)S(1)}, bf16[2,160,1024]{2,1,0:T(8,128)(2,1)S(1)}, u32[]{:S(2)}, u32[]{:S(2)}) collective-permute-start(bf16[2,160,1024]{2,1,0:T(8,128)(2,1)S(1)} %pad_maximum_fusion.1.refs_0_), channel_id=1, source_target_pairs={{0,192},{64,128},{128,64},{192,0},{32,96},{96,32},{160,224},{224,1... | collective-permute-start | bytes 1966088 | tf_op jit(solution)/shard_map/ppermute | solution.py:27
  194.3 11.6 %collective-permute-start.12 = (bf16[2,160,1024]{2,1,0:T(8,128)(2,1)S(1)}, bf16[2,160,1024]{2,1,0:T(8,128)(2,1)S(1)}, u32[]{:S(2)}, u32[]{:S(2)}) collective-permute-start(bf16[2,160,1024]{2,1,0:T(8,128)(2,1)S(1)} %pad_maximum_fusion.1.refs_0_), channel_id=1, source_target_pairs={{0,32},{32,0},{1,33},{33,1},{2,34},{34,2},{3,35},{35,3},{4,36},{36... | collective-permute-start | bytes 1966088 | tf_op jit(solution)/shard_map/ppermute | solution.py:31
  205.9 2.2 collective-permute-start.13
  217.3 64.1 %all-to-all-start.3 = ((bf16[32,40,896]{2,1,0:T(8,128)(2,1)}), bf16[32,40,896]{2,1,0:T(8,128)(2,1)}, u32[]{:S(2)}, u32[]{:S(2)}) async-start(bf16[32,40,896]{2,1,0:T(8,128)(2,1)} %bitcast.45), calls=%async_computation.3 | async-start | bytes 4587520 | tf_op jit(solution)/shard_map/all_to_all | solution.py:40
  233.8 8.0 %collective-permute-start.14 = (f32[32,128]{1,0:T(8,128)}, f32[32,128]{1,0:T(8,128)S(1)}, u32[]{:S(2)}, u32[]{:S(2)}) collective-permute-start(f32[32,128]{1,0:T(8,128)} %gate_terms.1), channel_id=1, source_target_pairs={{0,32},{32,0},{1,33},{33,1},{2,34},{34,2},{3,35},{35,3},{4,36},{36... | collective-permute-start | bytes 49160 | tf_op jit(solution)/shard_map/ppermute | solution.py:31
  241.9 6.7 %collective-permute-start.15 = (f32[32,128]{1,0:T(8,128)S(1)}, f32[32,128]{1,0:T(8,128)S(1)}, u32[]{:S(2)}, u32[]{:S(2)}) collective-permute-start(f32[32,128]{1,0:T(8,128)S(1)} %add.102), channel_id=1, source_target_pairs={{0,64},{64,0},{128,192},{192,128},{32,96},{96,32},{160,224},{224,1... | collective-permute-start | bytes 49160 | tf_op jit(solution)/shard_map/ppermute | solution.py:27
  248.6 5.0 %collective-permute-start.16 = (f32[32,128]{1,0:T(8,128)S(1)}, f32[32,128]{1,0:T(8,128)S(1)}, u32[]{:S(2)}, u32[]{:S(2)}) collective-permute-start(f32[32,128]{1,0:T(8,128)S(1)} %add.103), channel_id=1, source_target_pairs={{0,192},{64,128},{128,64},{192,0},{32,224},{96,160},{160,96},{224,... | collective-permute-start | bytes 49160 | tf_op jit(solution)/shard_map/ppermute | solution.py:27
  (13 other events, 76.3 us)

commit v2 on v1

--- a/solution.py
+++ b/solution.py
@@ -192,71 +192,78 @@
     )(table, weight, slot_rows.reshape(NY, 2, rows, width))
 
 
-def expand_rows(table, shares, weight, contract):
-    rows = shares[0].shape[1]
-    hid, width = weight.shape[contract], weight.shape[1 - contract]
-
-    def kernel(table_ref, weight_ref, *refs):
-        ins, (out, joined, held, made, held_weight, in_sems, out_sems, join_sems, weight_sem) = (
-            refs[:4], refs[4:]
-        )
+def expand_rows(table, offset, own, other, weight, contract, made_before=()):
+    rows, hid = own.shape[1:]
+    width = weight.shape[1 - contract]
+    shapes = [
+        jax.ShapeDtypeStruct((NY, 2, rows, width), BF),
+        jax.ShapeDtypeStruct((NY, 2, rows, hid), BF),
+    ]
+
+    def kernel(table_ref, weight_ref, own_ref, other_ref, *refs):
+        refs = refs[len(made_before) :]
+        out, joined, held, made, held_weight, in_sems, out_sems, join_sems, weight_sem = refs
         core = table_ref[4 * NY]
         fetch = pltpu.make_async_copy(weight_ref, held_weight, weight_sem)
-        fetch.start()
-        for n in range(4):
+        gets = [
+            pltpu.make_async_copy(ref, held.at[n], in_sems.at[n])
+            for n, ref in enumerate((own_ref, other_ref))
+        ]
+        for c in (*gets, fetch):
+            c.start()
+
+        def place(n, m):
+            return table_ref[offset + NY * n + m], jnp.where(n == 0, core, 1 - core)
+
+        def put(n, m):
+            at, half = place(n, m)
+            return pltpu.make_async_copy(
+                made.at[n, pl.ds(m * rows, rows)], out.at[at, half], out_sems.at[n, m]
+            )
+
+        def keep(n, m):
+            at, half = place(n, m)
+            return pltpu.make_async_copy(held.at[n, m], joined.at[at, half], join_sems.at[n, m])
+
+        fetch.wait()
+
+        def step(n, carry):
+            pltpu.make_async_copy(own_ref, held.at[n], in_sems.at[n]).wait()
             for m in range(2):
-                place = table_ref[2 * NY + 2 * n + m]
-                half = core if n < 2 else 1 - core
-                pltpu.make_async_copy(
-                    ins[n].at[m], held.at[place, half], in_sems.at[place, half]
-                ).start()
-
-        def put(i):
-            return pltpu.make_async_copy(made.at[i], out.at[i], out_sems.at[i])
-
-        def keep(i):
-            return pltpu.make_async_copy(held.at[i], joined.at[i], join_sems.at[i])
-
-        fetch.wait()
-
-        def step(i, carry):
-            for h in range(2):
-                pltpu.make_async_copy(ins[0].at[0], held.at[i, h], in_sems.at[i, h]).wait()
-            keep(i).start()
-            made[i] = lax.dot_general(
-                held[i].reshape(2 * rows, hid), held_weight[...],
+                keep(n, m).start()
+            made[n] = lax.dot_general(
+                held[n].reshape(2 * rows, hid), held_weight[...],
                 (((1,), (contract,)), ((), ())), preferred_element_type=F32,
             ).astype(BF)
-            put(i).start()
+            for m in range(2):
+                put(n, m).start()
             return carry
 
-        lax.fori_loop(0, NY, step, 0)
-        for i in range(NY):
-            put(i).wait()
-            keep(i).wait()
-
-    out, joined = pl.pallas_call(
-        kernel,
-        out_shape=[
-            jax.ShapeDtypeStruct((NY, 2 * rows, width), BF),
-            jax.ShapeDtypeStruct((NY, 2, rows, hid), BF),
-        ],
-        in_specs=[SMEM, ANY] + [ANY] * 4,
+        lax.fori_loop(0, 2, step, 0)
+        for n in range(2):
+            for m in range(2):
+                put(n, m).wait()
+                keep(n, m).wait()
+
+    return pl.pallas_call(
+        kernel,
+        out_shape=shapes,
+        in_specs=[SMEM] + [ANY] * (3 + len(made_before)),
         out_specs=[ANY] * 2,
         scratch_shapes=[
-            pltpu.VMEM((NY, 2, rows, hid), BF),
-            pltpu.VMEM((NY, 2 * rows, width), BF),
+            pltpu.VMEM((2, 2, rows, hid), BF),
+            pltpu.VMEM((2, 2 * rows, width), BF),
             pltpu.VMEM(weight.shape, BF),
-            pltpu.SemaphoreType.DMA((NY, 2)),
-            pltpu.SemaphoreType.DMA((NY,)),
-            pltpu.SemaphoreType.DMA((NY,)),
+            pltpu.SemaphoreType.DMA((2,)),
+            pltpu.SemaphoreType.DMA((2, 2)),
+            pltpu.SemaphoreType.DMA((2, 2)),
             pltpu.SemaphoreType.DMA,
         ],
+        input_output_aliases={4: 0, 5: 1} if made_before else {},
         cost_estimate=pl.CostEstimate(
-            flops=2_400_000_000, bytes_accessed=9_000_000, transcendentals=0
+            flops=1_200_000_000, bytes_accessed=5_000_000, transcendentals=0
         ),
-    )(table, weight, *shares)
-    return out.reshape(NY * 2 * rows, width), joined.reshape(NY * 2 * rows, hid)
+    )(table, weight, own, other, *made_before)
 
 
 def weight_grads(left, right, step):
@@ -354,6 +361,7 @@
     slots = experts * cap
     y, core = lax.axis_index("y"), lax.axis_index("core")
     w_up, w_down = up_weight[0], down_weight[0]
+    hid = w_up.shape[1]
 
     side_y = 1 - 2 * ((y + core) % 2)
     turn = (jnp.arange(NY, dtype=jnp.int32) - y) % NY
@@ -410,12 +418,17 @@
 
     keep, away = partial_sums(table, tie(g_slots, hidden_shares[1]), w_down, 1)
     got, near, last, first = reduce(keep, away)
-    hidden_shares[0] = tie(hidden_shares[0], keep)
-    out_rows, hidden = expand_rows(table, hidden_shares, w_down, 0)
+    pair, far, other_pair, other_far = hidden_shares
+    begun = expand_rows(table, 2 * NY, pair, other_pair, w_down, 0)
+    out_rows, hidden = expand_rows(table, 2 * NY + 2, tie(far, keep), other_far, w_down, 0, begun)
+    out_rows, hidden = out_rows.reshape(slots, width), hidden.reshape(slots, hid)
     out_back = scatter(tie(out_rows, first))
 
     grads = spread(grad_share(keep, got, near, last, pre))
-    dx_rows, pre_grad = expand_rows(table, grads, w_up, 1)
+    pair, far, other_pair, other_far = grads
+    begun = expand_rows(table, 2 * NY, pair, other_pair, w_up, 1)
+    dx_rows, pre_grad = expand_rows(table, 2 * NY + 2, far, other_far, w_up, 1, begun)
+    dx_rows, pre_grad = dx_rows.reshape(slots, width), pre_grad.reshape(slots, hid)
     dx_back = scatter(tie(dx_rows, out_back))
 
     mixed = mix_rows((gate_hi.T, gate_lo.T), out_back)

time: 286 us -> 291 us (1.017)
  Pallas kernels: 66.3 us -> 72.6 us
    pallas_call x2 -> x4, Pallas kernels: 14.6 us -> 20.9 us  [expand_rows(): pl.pallas_call(kernel, out_shape=shapes, in_specs=[SMEM] + [ANY] * (3 + l...]
    unnamed x32 -> x34, local copies, waits for them, and re-layouts: 6.13 us -> 5.22 us
  transfers between devices with their start and end apart: 21 -> 21, of which waited for: 17 -> 14; matrix products, arithmetic and copies ran while one was open for 3% -> 3% of each run, Pallas kernels for 18% -> 20%
where the time goes in v2:
time: 291 us; the launch traced here: 290 us
  waiting for transfers between devices  161 us (55%)
  Pallas kernels  72.6 us (25%)
  starting transfers between devices  38.4 us (13%)
  local copies, waits for them, and re-layouts  8.55 us (3%)
  other arithmetic  8.25 us (3%)
    all_to_all x4, waiting for transfers between devices, scatter(): lax.all_to_all(parts, ('z', 'x'), split_axis=0, concat_axis=0, tiled=True)  78.5 us
    ppermute x10, waiting for transfers between devices, swap(): return lax.ppermute(value, ('y', 'core'), pairs)  75.5 us
    all_to_all x4, starting transfers between devices, scatter(): lax.all_to_all(parts, ('z', 'x'), split_axis=0, concat_axis=0, tiled=True)  34.5 us
    pallas_call x4, Pallas kernels, expand_rows(): pl.pallas_call(kernel, out_shape=shapes, in_specs=[SMEM] + [ANY] * (3 + l...  20.9 us
    pallas_call x2, Pallas kernels, partial_sums(): pl.pallas_call(kernel, grid=(hid // step,), out_shape=[jax.ShapeDtypeStru...  15.3 us
    pallas_call x2, Pallas kernels, weight_grads(): pl.pallas_call(kernel, grid=(count // step,), out_shape=jax.ShapeDtypeStr...  14.6 us
    ppermute x7, waiting for transfers between devices, swap_core(): return lax.ppermute(value, 'core', [(0, 1), (1, 0)])  6.8 us
    pallas_call x2, Pallas kernels, mix_rows(): pl.pallas_call(kernel, grid=(count,), out_shape=jax.ShapeDtypeStruct((tok...  6.26 us
  transfers between devices with their start and end apart: 21, of which 14 were waited for; matrix products, arithmetic and copies ran while one was open for 3% of the time, Pallas kernels for 20%

profile of v2, /device:TPU:24, one launch (start us, length us, event | category | flops | bytes accessed | tf_op | source)
XLA Modules:
  0.0 289.6 jit_solution(7594257547913300119)
XLA Ops:
  4.6 11.3 %all-to-all-start = ((bf16[32,40,896]{2,1,0:T(8,128)(2,1)}), bf16[32,40,896]{2,1,0:T(8,128)(2,1)S(1)}, u32[]{:S(2)}, u32[]{:S(2)}) async-start(bf16[32,40,896]{2,1,0:T(8,128)(2,1)} %bitcast.47), calls=%async_computation | async-start | bytes 4587520 | tf_op jit(solution)/shard_map/all_to_all | solution.py:40
  16.7 4.4 %select_scaled.1 = bf16[1280,896]{1,0:T(8,128)(2,1)} custom-call(bf16[1280,128]{1,0:T(8,128)(2,1)} %get-tuple-element.34.pick_ref, bf16[1280,128]{1,0:T(8,128)(2,1)} %get-tuple-element.29.refs_0_, bf16[1280,128]{1,0:T(8,128)(2,1)} %get-tuple-element.30.refs_1_, bf16[128,896]{1,0:T(8,128)(2,1)} %values_ref.1), custom_call_target="tpu_custom_call" | custom-call | flops 300000000 | bytes 3000000 | tf_op jit(solution)/shard_map/select_scaled/pallas_call | solution.py:59
  21.1 49.2 %all-to-all-done = bf16[32,40,896]{2,1,0:T(8,128)(2,1)S(1)} async-done(((bf16[32,40,896]{2,1,0:T(8,128)(2,1)}), bf16[32,40,896]{2,1,0:T(8,128)(2,1)S(1)}, u32[]{:S(2)}, u32[]{:S(2)}) %all-to-all-start) | async-done | bytes 2293792 | tf_op jit(solution)/shard_map/all_to_all | solution.py:40
  71.7 5.5 %all-to-all-start.1 = ((bf16[32,40,896]{2,1,0:T(8,128)(2,1)}), bf16[32,40,896]{2,1,0:T(8,128)(2,1)}, u32[]{:S(2)}, u32[]{:S(2)}) async-start(bf16[32,40,896]{2,1,0:T(8,128)(2,1)} %bitcast.40), calls=%async_computation.1 | async-start | bytes 4587520 | tf_op jit(solution)/shard_map/all_to_all | solution.py:40
  77.2 7.6 %shard_map.101 = (f32[4,160,1024]{2,1,0:T(8,128)}, bf16[4,160,1024]{2,1,0:T(8,128)(2,1)}) custom-call(s32[17]{0:T(128)} %concatenate.3.table_ref, bf16[896,1024]{1,0:T(8,128)(2,1)} %bitcast.51, bf16[4,2,160,896]{3,2,1,0:T(8,128)(2,1)} %bitcast.45), custom_call_target="tpu_custom_call" | custom-call | flops 2400000000 | bytes 9000000 | tf_op jit(solution)/shard_map/pallas_call | solution.py:180
  90.6 9.8 %collective-permute-done.1 = bf16[2,160,1024]{2,1,0:T(8,128)(2,1)S(1)} collective-permute-done((bf16[2,160,1024]{2,1,0:T(8,128)(2,1)S(1)}, bf16[2,160,1024]{2,1,0:T(8,128)(2,1)S(1)}, u32[]{:S(2)}, u32[]{:S(2)}) %collective-permute-start.1) | collective-permute-done | bytes 655392 | tf_op jit(solution)/shard_map/ppermute | solution.py:27
  100.9 8.1 %collective-permute-done.2 = bf16[160,1024]{1,0:T(8,128)(2,1)S(1)} collective-permute-done((bf16[160,1024]{1,0:T(8,128)(2,1)S(1)}, bf16[160,1024]{1,0:T(8,128)(2,1)S(1)}, u32[]{:S(2)}, u32[]{:S(2)}) %collective-permute-start.2) | collective-permute-done | bytes 327712 | tf_op jit(solution)/shard_map/ppermute | solution.py:27
  110.0 7.1 %collective-permute-done.3 = bf16[160,1024]{1,0:T(8,128)(2,1)S(1)} collective-permute-done((bf16[160,1024]{1,0:T(8,128)(2,1)S(1)}, bf16[160,1024]{1,0:T(8,128)(2,1)S(1)}, u32[]{:S(2)}, u32[]{:S(2)}) %collective-permute-start.3) | collective-permute-done | bytes 327712 | tf_op jit(solution)/shard_map/ppermute | solution.py:27
  117.5 11.6 %collective-permute-done.4.own_ref = bf16[2,160,1024]{2,1,0:T(8,128)(2,1)S(1)} collective-permute-done((bf16[2,160,1024]{2,1,0:T(8,128)(2,1)S(1)}, bf16[2,160,1024]{2,1,0:T(8,128)(2,1)S(1)}, u32[]{:S(2)}, u32[]{:S(2)}) %collective-permute-start.4) | collective-permute-done | bytes 655392 | tf_op jit(solution)/shard_map/ppermute | solution.py:27
  131.2 7.7 %shard_map.102 = (f32[4,160,1024]{2,1,0:T(8,128)}, bf16[4,160,1024]{2,1,0:T(8,128)(2,1)}) custom-call(s32[17]{0:T(128)} %concatenate.3.table_ref, bf16[1024,896]{1,0:T(8,128)(2,1)} %bitcast.48, bf16[4,2,160,896]{3,2,1,0:T(8,128)(2,1)} %bitcast.18.rows_ref), custom_call_target="tpu_custom_call" | custom-call | flops 2400000000 | bytes 9000000 | tf_op jit(solution)/shard_map/pallas_call | solution.py:180
  144.0 5.2 %shard_map.103 = (bf16[4,2,160,896]{3,2,1,0:T(8,128)(2,1)}, bf16[4,2,160,1024]{3,2,1,0:T(8,128)(2,1)}) custom-call(s32[17]{0:T(128)} %concatenate.3.table_ref, bf16[1024,896]{1,0:T(8,128)(2,1)} %bitcast.49, bf16[2,160,1024]{2,1,0:T(8,128)(2,1)} %copy-done.11, bf16[2,160,1024]{2,1,0:T(8,128)(2,1)} %copy-done.16), custom_call_target="tpu_custom_call" | custom-call | flops 1200000000 | bytes 5000000 | tf_op jit(solution)/shard_map/pallas_call | solution.py:248
  150.1 5.3 %shard_map.104 = (bf16[4,2,160,896]{3,2,1,0:T(8,128)(2,1)}, bf16[4,2,160,1024]{3,2,1,0:T(8,128)(2,1)}) custom-call(s32[17]{0:T(128)} %concatenate.3.table_ref, bf16[1024,896]{1,0:T(8,128)(2,1)} %bitcast.50, bf16[2,160,1024]{2,1,0:T(8,128)(2,1)} %copy-done.8, bf16[2,160,1024]{2,1,0:T(8,128)(2,1)} %copy-done.10, ...), custom_call_target="tpu_custom_call", output_to_operand_aliasing={{0}: (4, {}), {1}: (5, {})} | custom-call | flops 1200000000 | bytes 5000000 | tf_op jit(solution)/shard_map/pallas_call | solution.py:248
  157.5 7.8 %all-to-all-start.2 = ((bf16[32,40,896]{2,1,0:T(8,128)(2,1)}), bf16[32,40,896]{2,1,0:T(8,128)(2,1)S(1)}, u32[]{:S(2)}, u32[]{:S(2)}) async-start(bf16[32,40,896]{2,1,0:T(8,128)(2,1)} %bitcast.41), calls=%async_computation.2 | async-start | bytes 4587520 | tf_op jit(solution)/shard_map/all_to_all | solution.py:40
  165.4 10.8 %collective-permute-done.8.near_ref = bf16[2,160,1024]{2,1,0:T(8,128)(2,1)S(1)} collective-permute-done((bf16[2,160,1024]{2,1,0:T(8,128)(2,1)}, bf16[2,160,1024]{2,1,0:T(8,128)(2,1)S(1)}, u32[]{:S(2)}, u32[]{:S(2)}) %collective-permute-start.8) | collective-permute-done | bytes 655392 | tf_op jit(solution)/shard_map/ppermute | solution.py:27
  178.1 8.0 %collective-permute-done.9.last_ref = bf16[160,1024]{1,0:T(8,128)(2,1)S(1)} collective-permute-done((bf16[160,1024]{1,0:T(8,128)(2,1)S(1)}, bf16[160,1024]{1,0:T(8,128)(2,1)S(1)}, u32[]{:S(2)}, u32[]{:S(2)}) %collective-permute-start.9) | collective-permute-done | bytes 327712 | tf_op jit(solution)/shard_map/ppermute | solution.py:27
  189.6 7.3 %collective-permute-done.10 = bf16[160,1024]{1,0:T(8,128)(2,1)S(1)} collective-permute-done((bf16[160,1024]{1,0:T(8,128)(2,1)}, bf16[160,1024]{1,0:T(8,128)(2,1)S(1)}, u32[]{:S(2)}, u32[]{:S(2)}) %collective-permute-start.10) | collective-permute-done | bytes 327712 | tf_op jit(solution)/shard_map/ppermute | solution.py:27
  198.5 11.5 %collective-permute-done.11.own_ref = bf16[2,160,1024]{2,1,0:T(8,128)(2,1)S(1)} collective-permute-done((bf16[2,160,1024]{2,1,0:T(8,128)(2,1)S(1)}, bf16[2,160,1024]{2,1,0:T(8,128)(2,1)S(1)}, u32[]{:S(2)}, u32[]{:S(2)}) %collective-permute-start.11) | collective-permute-done | bytes 655392 | tf_op jit(solution)/shard_map/ppermute | solution.py:27
  210.0 5.2 %shard_map.106 = (bf16[4,2,160,896]{3,2,1,0:T(8,128)(2,1)}, bf16[4,2,160,1024]{3,2,1,0:T(8,128)(2,1)}) custom-call(s32[17]{0:T(128)} %concatenate.3.table_ref, bf16[896,1024]{1,0:T(8,128)(2,1)} %bitcast.52, bf16[2,160,1024]{2,1,0:T(8,128)(2,1)} %copy-done.12, bf16[2,160,1024]{2,1,0:T(8,128)(2,1)} %collective-permute-done.13.other_ref), custom_call_target="tpu_custom_call" | custom-call | flops 1200000000 | bytes 5000000 | tf_op jit(solution)/shard_map/pallas_call | solution.py:248
  215.3 5.2 %shard_map.107 = (bf16[4,2,160,896]{3,2,1,0:T(8,128)(2,1)}, bf16[4,2,160,1024]{3,2,1,0:T(8,128)(2,1)}) custom-call(s32[17]{0:T(128)} %concatenate.3.table_ref, bf16[896,1024]{1,0:T(8,128)(2,1)} %bitcast.53, bf16[2,160,1024]{2,1,0:T(8,128)(2,1)} %copy-done.9, ...), custom_call_target="tpu_custom_call", output_to_operand_aliasing={{0}: (4, {}), {1}: (5, {})} | custom-call | flops 1200000000 | bytes 5000000 | tf_op jit(solution)/shard_map/pallas_call | solution.py:248
  221.9 9.9 %all-to-all-start.3 = ((bf16[32,40,896]{2,1,0:T(8,128)(2,1)}), bf16[32,40,896]{2,1,0:T(8,128)(2,1)}, u32[]{:S(2)}, u32[]{:S(2)}) async-start(bf16[32,40,896]{2,1,0:T(8,128)(2,1)} %bitcast.42), calls=%async_computation.3 | async-start | bytes 4587520 | tf_op jit(solution)/shard_map/all_to_all | solution.py:40
  234.6 4.3 %gate_terms.1 = f32[32,128]{1,0:T(8,128)} custom-call(bf16[1280,128]{1,0:T(8,128)(2,1)} %get-tuple-element.34.pick_ref, bf16[1280,896]{1,0:T(8,128)(2,1)} %bitcast.38, bf16[128,896]{1,0:T(8,128)(2,1)} %values_ref.1), custom_call_target="tpu_custom_call" | custom-call | flops 300000000 | bytes 3000000 | tf_op jit(solution)/shard_map/gate_terms/pallas_call | solution.py:129
  239.1 8.0 %shard_map.109 = bf16[896,1024]{1,0:T(8,128)(2,1)} custom-call(bf16[1280,896]{1,0:T(8,128)(2,1)} %bitcast.46, bf16[1280,1024]{1,0:T(8,128)(2,1)} %bitcast.44), custom_call_target="tpu_custom_call" | custom-call | flops 2400000000 | bytes 7000000 | tf_op jit(solution)/shard_map/pallas_call | solution.py:278
  247.2 6.6 %shard_map.108 = bf16[1024,896]{1,0:T(8,128)(2,1)} custom-call(bf16[1280,1024]{1,0:T(8,128)(2,1)} %bitcast.43, bf16[1280,896]{1,0:T(8,128)(2,1)} %bitcast.17.right_ref), custom_call_target="tpu_custom_call" | custom-call | flops 2400000000 | bytes 7000000 | tf_op jit(solution)/shard_map/pallas_call | solution.py:278
  259.5 27.2 %all-to-all-done.3 = bf16[32,40,896]{2,1,0:T(8,128)(2,1)} async-done(((bf16[32,40,896]{2,1,0:T(8,128)(2,1)}), bf16[32,40,896]{2,1,0:T(8,128)(2,1)}, u32[]{:S(2)}, u32[]{:S(2)}) %all-to-all-start.3) | async-done | bytes 2293792 | tf_op jit(solution)/shard_map/all_to_all | solution.py:40
  (83 shorter events, 44.0 us)
Async XLA Ops:
  4.6 65.6 %all-to-all-start = ((bf16[32,40,896]{2,1,0:T(8,128)(2,1)}), bf16[32,40,896]{2,1,0:T(8,128)(2,1)S(1)}, u32[]{:S(2)}, u32[]{:S(2)}) async-start(bf16[32,40,896]{2,1,0:T(8,128)(2,1)} %bitcast.47), calls=%async_computation | async-start | bytes 4587520 | tf_op jit(solution)/shard_map/all_to_all | solution.py:40
  71.7 59.5 %all-to-all-start.1 = ((bf16[32,40,896]{2,1,0:T(8,128)(2,1)}), bf16[32,40,896]{2,1,0:T(8,128)(2,1)}, u32[]{:S(2)}, u32[]{:S(2)}) async-start(bf16[32,40,896]{2,1,0:T(8,128)(2,1)} %bitcast.40), calls=%async_computation.1 | async-start | bytes 4587520 | tf_op jit(solution)/shard_map/all_to_all | solution.py:40
  84.9 15.6 %copy-start.3 = (f32[4,160,1024]{2,1,0:T(8,128)S(1)}, f32[4,160,1024]{2,1,0:T(8,128)}, u32[]{:S(2)}) copy-start(f32[4,160,1024]{2,1,0:T(8,128)} %get-tuple-element.32) | copy-start | bytes 7864324
  84.9 3.3 %collective-permute-start = (bf16[4,160,1024]{2,1,0:T(8,128)(2,1)}, bf16[4,160,1024]{2,1,0:T(8,128)(2,1)S(1)}, u32[]{:S(2)}, u32[]{:S(2)}) collective-permute-start(bf16[4,160,1024]{2,1,0:T(8,128)(2,1)} %get-tuple-element.33), channel_id=1, source_target_pairs={{0,32},{32,0},{1,33},{33,1},{2,34},{34,2},{3,35},{35,3},{4,36},{36... | collective-permute-start | bytes 3932168 | tf_op jit(solution)/shard_map/ppermute | solution.py:31
  89.7 10.7 %collective-permute-start.1 = (bf16[2,160,1024]{2,1,0:T(8,128)(2,1)S(1)}, bf16[2,160,1024]{2,1,0:T(8,128)(2,1)S(1)}, u32[]{:S(2)}, u32[]{:S(2)}) collective-permute-start(bf16[2,160,1024]{2,1,0:T(8,128)(2,1)S(1)} %add_convert_fusion.1), channel_id=1, source_target_pairs={{0,64},{64,0},{128,192},{192,128},{32,224},{96,160},{160,96},{224,... | collective-permute-start | bytes 1966088 | tf_op jit(solution)/shard_map/ppermute | solution.py:27
  100.6 8.4 %collective-permute-start.2 = (bf16[160,1024]{1,0:T(8,128)(2,1)S(1)}, bf16[160,1024]{1,0:T(8,128)(2,1)S(1)}, u32[]{:S(2)}, u32[]{:S(2)}) collective-permute-start(bf16[160,1024]{1,0:T(8,128)(2,1)S(1)} %fusion), channel_id=1, source_target_pairs={{0,192},{64,128},{128,64},{192,0},{32,96},{96,32},{160,224},{224,1... | collective-permute-start | bytes 983048 | tf_op jit(solution)/shard_map/ppermute | solution.py:27
  110.0 7.1 %collective-permute-start.3 = (bf16[160,1024]{1,0:T(8,128)(2,1)S(1)}, bf16[160,1024]{1,0:T(8,128)(2,1)S(1)}, u32[]{:S(2)}, u32[]{:S(2)}) collective-permute-start(bf16[160,1024]{1,0:T(8,128)(2,1)S(1)} %get-tuple-element.53), channel_id=1, source_target_pairs={{0,64},{64,0},{128,192},{192,128},{32,224},{96,160},{160,96},{224,... | collective-permute-start | bytes 983048 | tf_op jit(solution)/shard_map/ppermute | solution.py:27
  117.2 21.9 %copy-start.11 = (bf16[2,160,1024]{2,1,0:T(8,128)(2,1)}, bf16[2,160,1024]{2,1,0:T(8,128)(2,1)S(1)}, u32[]{:S(2)}) copy-start(bf16[2,160,1024]{2,1,0:T(8,128)(2,1)S(1)} %pad_maximum_fusion.own_ref) | copy-start | bytes 1966084
  117.2 11.9 %collective-permute-start.4 = (bf16[2,160,1024]{2,1,0:T(8,128)(2,1)S(1)}, bf16[2,160,1024]{2,1,0:T(8,128)(2,1)S(1)}, u32[]{:S(2)}, u32[]{:S(2)}) collective-permute-start(bf16[2,160,1024]{2,1,0:T(8,128)(2,1)S(1)} %pad_maximum_fusion.own_ref), channel_id=1, source_target_pairs={{0,192},{64,128},{128,64},{192,0},{32,96},{96,32},{160,224},{224,1... | collective-permute-start | bytes 1966088 | tf_op jit(solution)/shard_map/ppermute | solution.py:27
  138.9 16.5 %collective-permute-start.7 = (bf16[4,160,1024]{2,1,0:T(8,128)(2,1)}, bf16[4,160,1024]{2,1,0:T(8,128)(2,1)}, u32[]{:S(2)}, u32[]{:S(2)}) collective-permute-start(bf16[4,160,1024]{2,1,0:T(8,128)(2,1)} %get-tuple-element.42), channel_id=1, source_target_pairs={{0,32},{32,0},{1,33},{33,1},{2,34},{34,2},{3,35},{35,3},{4,36},{36... | collective-permute-start | bytes 3932168 | tf_op jit(solution)/shard_map/ppermute | solution.py:31
  139.0 4.2 %collective-permute-start.6 = (bf16[2,160,1024]{2,1,0:T(8,128)(2,1)S(1)}, bf16[2,160,1024]{2,1,0:T(8,128)(2,1)S(1)}, u32[]{:S(2)}, u32[]{:S(2)}) collective-permute-start(bf16[2,160,1024]{2,1,0:T(8,128)(2,1)S(1)} %pad_maximum_fusion.own_ref), channel_id=1, source_target_pairs={{0,32},{32,0},{1,33},{33,1},{2,34},{34,2},{3,35},{35,3},{4,36},{36... | collective-permute-start | bytes 1966088 | tf_op jit(solution)/shard_map/ppermute | solution.py:31
  139.5 9.7 %collective-permute-start.5 = (bf16[2,160,1024]{2,1,0:T(8,128)(2,1)S(1)}, bf16[2,160,1024]{2,1,0:T(8,128)(2,1)S(1)}, u32[]{:S(2)}, u32[]{:S(2)}) collective-permute-start(bf16[2,160,1024]{2,1,0:T(8,128)(2,1)S(1)} %collective-permute-done.4.own_ref), channel_id=1, source_target_pairs={{0,32},{32,0},{1,33},{33,1},{2,34},{34,2},{3,35},{35,3},{4,36},{36... | collective-permute-start | bytes 1966088 | tf_op jit(solution)/shard_map/ppermute | solution.py:31
  157.5 63.0 %all-to-all-start.2 = ((bf16[32,40,896]{2,1,0:T(8,128)(2,1)}), bf16[32,40,896]{2,1,0:T(8,128)(2,1)S(1)}, u32[]{:S(2)}, u32[]{:S(2)}) async-start(bf16[32,40,896]{2,1,0:T(8,128)(2,1)} %bitcast.41), calls=%async_computation.2 | async-start | bytes 4587520 | tf_op jit(solution)/shard_map/all_to_all | solution.py:40
  165.3 10.9 %collective-permute-start.8 = (bf16[2,160,1024]{2,1,0:T(8,128)(2,1)}, bf16[2,160,1024]{2,1,0:T(8,128)(2,1)S(1)}, u32[]{:S(2)}, u32[]{:S(2)}) collective-permute-start(bf16[2,160,1024]{2,1,0:T(8,128)(2,1)} %add_convert_fusion), channel_id=1, source_target_pairs={{0,64},{64,0},{128,192},{192,128},{32,224},{96,160},{160,96},{224,... | collective-permute-start | bytes 1966088 | tf_op jit(solution)/shard_map/ppermute | solution.py:27
  177.7 8.4 %collective-permute-start.9 = (bf16[160,1024]{1,0:T(8,128)(2,1)S(1)}, bf16[160,1024]{1,0:T(8,128)(2,1)S(1)}, u32[]{:S(2)}, u32[]{:S(2)}) collective-permute-start(bf16[160,1024]{1,0:T(8,128)(2,1)S(1)} %fusion.1), channel_id=1, source_target_pairs={{0,192},{64,128},{128,64},{192,0},{32,96},{96,32},{160,224},{224,1... | collective-permute-start | bytes 983048 | tf_op jit(solution)/shard_map/ppermute | solution.py:27
  189.6 7.3 %collective-permute-start.10 = (bf16[160,1024]{1,0:T(8,128)(2,1)}, bf16[160,1024]{1,0:T(8,128)(2,1)S(1)}, u32[]{:S(2)}, u32[]{:S(2)}) collective-permute-start(bf16[160,1024]{1,0:T(8,128)(2,1)} %grad_share.1), channel_id=1, source_target_pairs={{0,64},{64,0},{128,192},{192,128},{32,224},{96,160},{160,96},{224,... | collective-permute-start | bytes 983048 | tf_op jit(solution)/shard_map/ppermute | solution.py:27
  197.9 12.1 %collective-permute-start.11 = (bf16[2,160,1024]{2,1,0:T(8,128)(2,1)S(1)}, bf16[2,160,1024]{2,1,0:T(8,128)(2,1)S(1)}, u32[]{:S(2)}, u32[]{:S(2)}) collective-permute-start(bf16[2,160,1024]{2,1,0:T(8,128)(2,1)S(1)} %pad_maximum_fusion.1.own_ref), channel_id=1, source_target_pairs={{0,192},{64,128},{128,64},{192,0},{32,96},{96,32},{160,224},{224,1... | collective-permute-start | bytes 1966088 | tf_op jit(solution)/shard_map/ppermute | solution.py:27
  198.5 11.6 %collective-permute-start.13 = (bf16[2,160,1024]{2,1,0:T(8,128)(2,1)S(1)}, bf16[2,160,1024]{2,1,0:T(8,128)(2,1)}, u32[]{:S(2)}, u32[]{:S(2)}) collective-permute-start(bf16[2,160,1024]{2,1,0:T(8,128)(2,1)S(1)} %pad_maximum_fusion.1.own_ref), channel_id=1, source_target_pairs={{0,32},{32,0},{1,33},{33,1},{2,34},{34,2},{3,35},{35,3},{4,36},{36... | collective-permute-start | bytes 1966088 | tf_op jit(solution)/shard_map/ppermute | solution.py:31
  210.0 5.3 %collective-permute-start.12 = (bf16[2,160,1024]{2,1,0:T(8,128)(2,1)S(1)}, bf16[2,160,1024]{2,1,0:T(8,128)(2,1)}, u32[]{:S(2)}, u32[]{:S(2)}) collective-permute-start(bf16[2,160,1024]{2,1,0:T(8,128)(2,1)S(1)} %collective-permute-done.11.own_ref), channel_id=1, source_target_pairs={{0,32},{32,0},{1,33},{33,1},{2,34},{34,2},{3,35},{35,3},{4,36},{36... | collective-permute-start | bytes 1966088 | tf_op jit(solution)/shard_map/ppermute | solution.py:31
  220.6 13.1 %copy-start.2 = (bf16[1280,128]{1,0:T(8,128)(2,1)S(1)}, bf16[1280,128]{1,0:T(8,128)(2,1)}, u32[]{:S(2)}) copy-start(bf16[1280,128]{1,0:T(8,128)(2,1)} %get-tuple-element.34.pick_ref) | copy-start | bytes 983044
  221.9 64.8 %all-to-all-start.3 = ((bf16[32,40,896]{2,1,0:T(8,128)(2,1)}), bf16[32,40,896]{2,1,0:T(8,128)(2,1)}, u32[]{:S(2)}, u32[]{:S(2)}) async-start(bf16[32,40,896]{2,1,0:T(8,128)(2,1)} %bitcast.42), calls=%async_computation.3 | async-start | bytes 4587520 | tf_op jit(solution)/shard_map/all_to_all | solution.py:40
  238.9 8.3 %collective-permute-start.14 = (f32[32,128]{1,0:T(8,128)}, f32[32,128]{1,0:T(8,128)S(1)}, u32[]{:S(2)}, u32[]{:S(2)}) collective-permute-start(f32[32,128]{1,0:T(8,128)} %gate_terms.1), channel_id=1, source_target_pairs={{0,32},{32,0},{1,33},{33,1},{2,34},{34,2},{3,35},{35,3},{4,36},{36... | collective-permute-start | bytes 49160 | tf_op jit(solution)/shard_map/ppermute | solution.py:31
  247.1 6.7 %collective-permute-start.15 = (f32[32,128]{1,0:T(8,128)S(1)}, f32[32,128]{1,0:T(8,128)S(1)}, u32[]{:S(2)}, u32[]{:S(2)}) collective-permute-start(f32[32,128]{1,0:T(8,128)S(1)} %add.102), channel_id=1, source_target_pairs={{0,64},{64,0},{128,192},{192,128},{32,96},{96,32},{160,224},{224,1... | collective-permute-start | bytes 49160 | tf_op jit(solution)/shard_map/ppermute | solution.py:27
  253.9 5.0 %collective-permute-start.16 = (f32[32,128]{1,0:T(8,128)S(1)}, f32[32,128]{1,0:T(8,128)S(1)}, u32[]{:S(2)}, u32[]{:S(2)}) collective-permute-start(f32[32,128]{1,0:T(8,128)S(1)} %add.103), channel_id=1, source_target_pairs={{0,192},{64,128},{128,64},{192,0},{32,224},{96,160},{160,96},{224,... | collective-permute-start | bytes 49160 | tf_op jit(solution)/shard_map/ppermute | solution.py:27
  (14 other events, 84.8 us)

commit v3 on v2

--- a/solution.py
+++ b/solution.py
@@ -11,6 +11,7 @@
 
 NZ, NX, NY = 8, 4, 4
 CHUNKS = 4
+FULL = 67_043_328
 
 
 ANY = pl.BlockSpec(memory_space=pl.ANY)
@@ -63,6 +64,7 @@
         in_specs=[chunk] * (1 + len(weights)) + [pl.BlockSpec((tok, width), lambda k: (0, 0))],
         out_specs=pl.BlockSpec((step, width), lambda k: (k, 0)),
         cost_estimate=pl.CostEstimate(flops=300_000_000, bytes_accessed=3_000_000, transcendentals=0),
+        compiler_params=pltpu.CompilerParams(vmem_limit_bytes=FULL),
         name="select_scaled" if weights else "select_plain",
     )(pick, *weights, values)
 
@@ -189,6 +191,7 @@
         cost_estimate=pl.CostEstimate(
             flops=2_400_000_000, bytes_accessed=9_000_000, transcendentals=0
         ),
+        compiler_params=pltpu.CompilerParams(vmem_limit_bytes=FULL),
     )(table, weight, slot_rows.reshape(NY, 2, rows, width))
 
 
@@ -287,6 +290,7 @@
         cost_estimate=pl.CostEstimate(
             flops=2_400_000_000, bytes_accessed=7_000_000, transcendentals=0
         ),
+        compiler_params=pltpu.CompilerParams(vmem_limit_bytes=FULL),
     )(left, right)
 
 
@@ -349,6 +353,7 @@
         ],
         out_specs=pl.BlockSpec((rows, hid), lambda n: (0, 0)),
         cost_estimate=pl.CostEstimate(flops=3_000_000, bytes_accessed=3_000_000, transcendentals=200_000),
+        compiler_params=pltpu.CompilerParams(vmem_limit_bytes=FULL),
         name="grad_share",
     )(keep, got, near, last, pre)
 

time: 291 us -> 289 us (level)
  waiting for transfers between devices: 161 us -> 158 us
  transfers between devices with their start and end apart: 21 -> 21, of which waited for: 14 -> 14; matrix products, arithmetic and copies ran while one was open for 3% -> 4% of each run, Pallas kernels for 20% -> 20%
where the time goes in v3:
time: 289 us; the launch traced here: 288 us
  waiting for transfers between devices  158 us (55%)
  Pallas kernels  72.5 us (25%)
  starting transfers between devices  39 us (13%)
  other arithmetic  9.26 us (3%)
  local copies, waits for them, and re-layouts  7.63 us (3%)
    all_to_all x4, waiting for transfers between devices, scatter(): lax.all_to_all(parts, ('z', 'x'), split_axis=0, concat_axis=0, tiled=True)  75.8 us
    ppermute x10, waiting for transfers between devices, swap(): return lax.ppermute(value, ('y', 'core'), pairs)  75.5 us
    all_to_all x4, starting transfers between devices, scatter(): lax.all_to_all(parts, ('z', 'x'), split_axis=0, concat_axis=0, tiled=True)  35.5 us
    pallas_call x4, Pallas kernels, expand_rows(): pl.pallas_call(kernel, out_shape=shapes, in_specs=[SMEM] + [ANY] * (3 + l...  20.9 us
    pallas_call x2, Pallas kernels, partial_sums(): pl.pallas_call(kernel, grid=(hid // step,), out_shape=[jax.ShapeDtypeStru...  15.3 us
    pallas_call x2, Pallas kernels, weight_grads(): pl.pallas_call(kernel, grid=(count // step,), out_shape=jax.ShapeDtypeStr...  14.6 us
    ppermute x7, waiting for transfers between devices, swap_core(): return lax.ppermute(value, 'core', [(0, 1), (1, 0)])  6.82 us
    pallas_call x2, Pallas kernels, mix_rows(): pl.pallas_call(kernel, grid=(count,), out_shape=jax.ShapeDtypeStruct((tok...  6.26 us
  transfers between devices with their start and end apart: 21, of which 14 were waited for; matrix products, arithmetic and copies ran while one was open for 4% of the time, Pallas kernels for 20%

profile of v3, /device:TPU:24, one launch (start us, length us, event | category | flops | bytes accessed | tf_op | source)
XLA Modules:
  0.0 287.6 jit_solution(5710532228056518547)
XLA Ops:
  4.6 11.4 %all-to-all-start = ((bf16[32,40,896]{2,1,0:T(8,128)(2,1)}), bf16[32,40,896]{2,1,0:T(8,128)(2,1)}, u32[]{:S(2)}, u32[]{:S(2)}) async-start(bf16[32,40,896]{2,1,0:T(8,128)(2,1)} %bitcast.42), calls=%async_computation | async-start | bytes 4587520 | tf_op jit(solution)/shard_map/all_to_all | solution.py:41
  16.8 4.4 %select_scaled.1 = bf16[1280,896]{1,0:T(8,128)(2,1)} custom-call(bf16[1280,128]{1,0:T(8,128)(2,1)} %get-tuple-element.34.pick_ref, bf16[1280,128]{1,0:T(8,128)(2,1)} %get-tuple-element.29.refs_0_, bf16[1280,128]{1,0:T(8,128)(2,1)} %get-tuple-element.30.refs_1_, bf16[128,896]{1,0:T(8,128)(2,1)} %values_ref.1), custom_call_target="tpu_custom_call" | custom-call | flops 300000000 | bytes 3000000 | tf_op jit(solution)/shard_map/select_scaled/pallas_call | solution.py:60
  21.2 49.2 %all-to-all-done = bf16[32,40,896]{2,1,0:T(8,128)(2,1)} async-done(((bf16[32,40,896]{2,1,0:T(8,128)(2,1)}), bf16[32,40,896]{2,1,0:T(8,128)(2,1)}, u32[]{:S(2)}, u32[]{:S(2)}) %all-to-all-start) | async-done | bytes 2293792 | tf_op jit(solution)/shard_map/all_to_all | solution.py:41
  70.4 5.5 %all-to-all-start.1 = ((bf16[32,40,896]{2,1,0:T(8,128)(2,1)}), bf16[32,40,896]{2,1,0:T(8,128)(2,1)}, u32[]{:S(2)}, u32[]{:S(2)}) async-start(bf16[32,40,896]{2,1,0:T(8,128)(2,1)} %bitcast.38), calls=%async_computation.1 | async-start | bytes 4587520 | tf_op jit(solution)/shard_map/all_to_all | solution.py:41
  75.9 7.6 %shard_map.101 = (f32[4,160,1024]{2,1,0:T(8,128)}, bf16[4,160,1024]{2,1,0:T(8,128)(2,1)}) custom-call(s32[17]{0:T(128)} %concatenate.3.table_ref, bf16[896,1024]{1,0:T(8,128)(2,1)} %bitcast.46, bf16[4,2,160,896]{3,2,1,0:T(8,128)(2,1)} %bitcast.10.rows_ref), custom_call_target="tpu_custom_call" | custom-call | flops 2400000000 | bytes 9000000 | tf_op jit(solution)/shard_map/pallas_call | solution.py:182
  89.2 9.8 %collective-permute-done.1 = bf16[2,160,1024]{2,1,0:T(8,128)(2,1)S(1)} collective-permute-done((bf16[2,160,1024]{2,1,0:T(8,128)(2,1)S(1)}, bf16[2,160,1024]{2,1,0:T(8,128)(2,1)S(1)}, u32[]{:S(2)}, u32[]{:S(2)}) %collective-permute-start.1) | collective-permute-done | bytes 655392 | tf_op jit(solution)/shard_map/ppermute | solution.py:28
  99.5 8.1 %collective-permute-done.2 = bf16[160,1024]{1,0:T(8,128)(2,1)S(1)} collective-permute-done((bf16[160,1024]{1,0:T(8,128)(2,1)S(1)}, bf16[160,1024]{1,0:T(8,128)(2,1)S(1)}, u32[]{:S(2)}, u32[]{:S(2)}) %collective-permute-start.2) | collective-permute-done | bytes 327712 | tf_op jit(solution)/shard_map/ppermute | solution.py:28
  108.7 7.1 %collective-permute-done.3 = bf16[160,1024]{1,0:T(8,128)(2,1)S(1)} collective-permute-done((bf16[160,1024]{1,0:T(8,128)(2,1)S(1)}, bf16[160,1024]{1,0:T(8,128)(2,1)S(1)}, u32[]{:S(2)}, u32[]{:S(2)}) %collective-permute-start.3) | collective-permute-done | bytes 327712 | tf_op jit(solution)/shard_map/ppermute | solution.py:28
  116.9 11.7 %collective-permute-done.4.own_ref = bf16[2,160,1024]{2,1,0:T(8,128)(2,1)} collective-permute-done((bf16[2,160,1024]{2,1,0:T(8,128)(2,1)S(1)}, bf16[2,160,1024]{2,1,0:T(8,128)(2,1)}, u32[]{:S(2)}, u32[]{:S(2)}) %collective-permute-start.4) | collective-permute-done | bytes 655392 | tf_op jit(solution)/shard_map/ppermute | solution.py:28
  129.9 7.7 %shard_map.102 = (f32[4,160,1024]{2,1,0:T(8,128)}, bf16[4,160,1024]{2,1,0:T(8,128)(2,1)}) custom-call(s32[17]{0:T(128)} %concatenate.3.table_ref, bf16[1024,896]{1,0:T(8,128)(2,1)} %bitcast.43, bf16[4,2,160,896]{3,2,1,0:T(8,128)(2,1)} %bitcast.18.rows_ref), custom_call_target="tpu_custom_call" | custom-call | flops 2400000000 | bytes 9000000 | tf_op jit(solution)/shard_map/pallas_call | solution.py:182
  142.7 5.2 %shard_map.103 = (bf16[4,2,160,896]{3,2,1,0:T(8,128)(2,1)}, bf16[4,2,160,1024]{3,2,1,0:T(8,128)(2,1)}) custom-call(s32[17]{0:T(128)} %concatenate.3.table_ref, bf16[1024,896]{1,0:T(8,128)(2,1)} %bitcast.44, bf16[2,160,1024]{2,1,0:T(8,128)(2,1)} %copy-done.9, bf16[2,160,1024]{2,1,0:T(8,128)(2,1)} %copy-done.13), custom_call_target="tpu_custom_call" | custom-call | flops 1200000000 | bytes 5000000 | tf_op jit(solution)/shard_map/pallas_call | solution.py:251
  148.8 5.3 %shard_map.104 = (bf16[4,2,160,896]{3,2,1,0:T(8,128)(2,1)}, bf16[4,2,160,1024]{3,2,1,0:T(8,128)(2,1)}) custom-call(s32[17]{0:T(128)} %concatenate.3.table_ref, bf16[1024,896]{1,0:T(8,128)(2,1)} %bitcast.45, bf16[2,160,1024]{2,1,0:T(8,128)(2,1)} %collective-permute-done.4.own_ref, ...), custom_call_target="tpu_custom_call", output_to_operand_aliasing={{0}: (4, {}), {1}: (5, {})} | custom-call | flops 1200000000 | bytes 5000000 | tf_op jit(solution)/shard_map/pallas_call | solution.py:251
  155.4 8.5 %all-to-all-start.2 = ((bf16[32,40,896]{2,1,0:T(8,128)(2,1)}), bf16[32,40,896]{2,1,0:T(8,128)(2,1)}, u32[]{:S(2)}, u32[]{:S(2)}) async-start(bf16[32,40,896]{2,1,0:T(8,128)(2,1)} %bitcast.20), calls=%async_computation.2 | async-start | bytes 4587520 | tf_op jit(solution)/shard_map/all_to_all | solution.py:41
  164.0 10.6 %collective-permute-done.8.near_ref = bf16[2,160,1024]{2,1,0:T(8,128)(2,1)S(1)} collective-permute-done((bf16[2,160,1024]{2,1,0:T(8,128)(2,1)S(1)}, bf16[2,160,1024]{2,1,0:T(8,128)(2,1)S(1)}, u32[]{:S(2)}, u32[]{:S(2)}) %collective-permute-start.8) | collective-permute-done | bytes 655392 | tf_op jit(solution)/shard_map/ppermute | solution.py:28
  176.2 8.1 %collective-permute-done.9.last_ref = bf16[160,1024]{1,0:T(8,128)(2,1)} collective-permute-done((bf16[160,1024]{1,0:T(8,128)(2,1)S(1)}, bf16[160,1024]{1,0:T(8,128)(2,1)}, u32[]{:S(2)}, u32[]{:S(2)}) %collective-permute-start.9) | collective-permute-done | bytes 327712 | tf_op jit(solution)/shard_map/ppermute | solution.py:28
  187.2 7.3 %collective-permute-done.10 = bf16[160,1024]{1,0:T(8,128)(2,1)S(1)} collective-permute-done((bf16[160,1024]{1,0:T(8,128)(2,1)}, bf16[160,1024]{1,0:T(8,128)(2,1)S(1)}, u32[]{:S(2)}, u32[]{:S(2)}) %collective-permute-start.10) | collective-permute-done | bytes 327712 | tf_op jit(solution)/shard_map/ppermute | solution.py:28
  196.0 11.5 %collective-permute-done.11.own_ref = bf16[2,160,1024]{2,1,0:T(8,128)(2,1)S(1)} collective-permute-done((bf16[2,160,1024]{2,1,0:T(8,128)(2,1)S(1)}, bf16[2,160,1024]{2,1,0:T(8,128)(2,1)S(1)}, u32[]{:S(2)}, u32[]{:S(2)}) %collective-permute-start.11) | collective-permute-done | bytes 655392 | tf_op jit(solution)/shard_map/ppermute | solution.py:28
  208.5 5.2 %shard_map.106 = (bf16[4,2,160,896]{3,2,1,0:T(8,128)(2,1)}, bf16[4,2,160,1024]{3,2,1,0:T(8,128)(2,1)}) custom-call(s32[17]{0:T(128)} %concatenate.3.table_ref, bf16[896,1024]{1,0:T(8,128)(2,1)} %bitcast.47, bf16[2,160,1024]{2,1,0:T(8,128)(2,1)} %copy-done.10, bf16[2,160,1024]{2,1,0:T(8,128)(2,1)} %copy-done.12), custom_call_target="tpu_custom_call" | custom-call | flops 1200000000 | bytes 5000000 | tf_op jit(solution)/shard_map/pallas_call | solution.py:251
  214.6 5.2 %shard_map.107 = (bf16[4,2,160,896]{3,2,1,0:T(8,128)(2,1)}, bf16[4,2,160,1024]{3,2,1,0:T(8,128)(2,1)}) custom-call(s32[17]{0:T(128)} %concatenate.3.table_ref, bf16[896,1024]{1,0:T(8,128)(2,1)} %bitcast.48, bf16[2,160,1024]{2,1,0:T(8,128)(2,1)} %copy-done.6, bf16[2,160,1024]{2,1,0:T(8,128)(2,1)} %copy-done.8, ...), custom_call_target="tpu_custom_call", output_to_operand_aliasing={{0}: (4, {}), {1}: (5, {})} | custom-call | flops 1200000000 | bytes 5000000 | tf_op jit(solution)/shard_map/pallas_call | solution.py:251
  219.9 10.0 %all-to-all-start.3 = ((bf16[32,40,896]{2,1,0:T(8,128)(2,1)}), bf16[32,40,896]{2,1,0:T(8,128)(2,1)}, u32[]{:S(2)}, u32[]{:S(2)}) async-start(bf16[32,40,896]{2,1,0:T(8,128)(2,1)} %bitcast.39), calls=%async_computation.3 | async-start | bytes 4587520 | tf_op jit(solution)/shard_map/all_to_all | solution.py:41
  232.6 4.3 %gate_terms.1 = f32[32,128]{1,0:T(8,128)} custom-call(bf16[1280,128]{1,0:T(8,128)(2,1)} %get-tuple-element.34.pick_ref, bf16[1280,896]{1,0:T(8,128)(2,1)} %bitcast.21.refs_2_.rows_ref, bf16[128,896]{1,0:T(8,128)(2,1)} %values_ref.1), custom_call_target="tpu_custom_call" | custom-call | flops 300000000 | bytes 3000000 | tf_op jit(solution)/shard_map/gate_terms/pallas_call | solution.py:131
  237.1 8.0 %shard_map.109 = bf16[896,1024]{1,0:T(8,128)(2,1)} custom-call(bf16[1280,896]{1,0:T(8,128)(2,1)} %bitcast.15.left_ref, bf16[1280,1024]{1,0:T(8,128)(2,1)} %bitcast.41), custom_call_target="tpu_custom_call" | custom-call | flops 2400000000 | bytes 7000000 | tf_op jit(solution)/shard_map/pallas_call | solution.py:281
  246.4 6.6 %shard_map.108 = bf16[1024,896]{1,0:T(8,128)(2,1)} custom-call(bf16[1280,1024]{1,0:T(8,128)(2,1)} %bitcast.40, bf16[1280,896]{1,0:T(8,128)(2,1)} %bitcast.17.right_ref), custom_call_target="tpu_custom_call" | custom-call | flops 2400000000 | bytes 7000000 | tf_op jit(solution)/shard_map/pallas_call | solution.py:281
  259.4 25.3 %all-to-all-done.3 = bf16[32,40,896]{2,1,0:T(8,128)(2,1)} async-done(((bf16[32,40,896]{2,1,0:T(8,128)(2,1)}), bf16[32,40,896]{2,1,0:T(8,128)(2,1)}, u32[]{:S(2)}, u32[]{:S(2)}) %all-to-all-start.3) | async-done | bytes 2293792 | tf_op jit(solution)/shard_map/all_to_all | solution.py:41
  (77 shorter events, 43.0 us)
Async XLA Ops:
  4.6 65.7 %all-to-all-start = ((bf16[32,40,896]{2,1,0:T(8,128)(2,1)}), bf16[32,40,896]{2,1,0:T(8,128)(2,1)}, u32[]{:S(2)}, u32[]{:S(2)}) async-start(bf16[32,40,896]{2,1,0:T(8,128)(2,1)} %bitcast.42), calls=%async_computation | async-start | bytes 4587520 | tf_op jit(solution)/shard_map/all_to_all | solution.py:41
  70.4 59.5 %all-to-all-start.1 = ((bf16[32,40,896]{2,1,0:T(8,128)(2,1)}), bf16[32,40,896]{2,1,0:T(8,128)(2,1)}, u32[]{:S(2)}, u32[]{:S(2)}) async-start(bf16[32,40,896]{2,1,0:T(8,128)(2,1)} %bitcast.38), calls=%async_computation.1 | async-start | bytes 4587520 | tf_op jit(solution)/shard_map/all_to_all | solution.py:41
  83.5 15.6 %copy-start.2 = (f32[4,160,1024]{2,1,0:T(8,128)S(1)}, f32[4,160,1024]{2,1,0:T(8,128)}, u32[]{:S(2)}) copy-start(f32[4,160,1024]{2,1,0:T(8,128)} %get-tuple-element.32) | copy-start | bytes 7864324
  83.5 3.3 %collective-permute-start = (bf16[4,160,1024]{2,1,0:T(8,128)(2,1)}, bf16[4,160,1024]{2,1,0:T(8,128)(2,1)S(1)}, u32[]{:S(2)}, u32[]{:S(2)}) collective-permute-start(bf16[4,160,1024]{2,1,0:T(8,128)(2,1)} %get-tuple-element.33), channel_id=1, source_target_pairs={{0,32},{32,0},{1,33},{33,1},{2,34},{34,2},{3,35},{35,3},{4,36},{36... | collective-permute-start | bytes 3932168 | tf_op jit(solution)/shard_map/ppermute | solution.py:32
  88.4 10.7 %collective-permute-start.1 = (bf16[2,160,1024]{2,1,0:T(8,128)(2,1)S(1)}, bf16[2,160,1024]{2,1,0:T(8,128)(2,1)S(1)}, u32[]{:S(2)}, u32[]{:S(2)}) collective-permute-start(bf16[2,160,1024]{2,1,0:T(8,128)(2,1)S(1)} %add_convert_fusion.1), channel_id=1, source_target_pairs={{0,64},{64,0},{128,192},{192,128},{32,224},{96,160},{160,96},{224,... | collective-permute-start | bytes 1966088 | tf_op jit(solution)/shard_map/ppermute | solution.py:28
  99.2 8.4 %collective-permute-start.2 = (bf16[160,1024]{1,0:T(8,128)(2,1)S(1)}, bf16[160,1024]{1,0:T(8,128)(2,1)S(1)}, u32[]{:S(2)}, u32[]{:S(2)}) collective-permute-start(bf16[160,1024]{1,0:T(8,128)(2,1)S(1)} %fusion), channel_id=1, source_target_pairs={{0,192},{64,128},{128,64},{192,0},{32,96},{96,32},{160,224},{224,1... | collective-permute-start | bytes 983048 | tf_op jit(solution)/shard_map/ppermute | solution.py:28
  108.7 7.1 %collective-permute-start.3 = (bf16[160,1024]{1,0:T(8,128)(2,1)S(1)}, bf16[160,1024]{1,0:T(8,128)(2,1)S(1)}, u32[]{:S(2)}, u32[]{:S(2)}) collective-permute-start(bf16[160,1024]{1,0:T(8,128)(2,1)S(1)} %get-tuple-element.53), channel_id=1, source_target_pairs={{0,64},{64,0},{128,192},{192,128},{32,224},{96,160},{160,96},{224,... | collective-permute-start | bytes 983048 | tf_op jit(solution)/shard_map/ppermute | solution.py:28
  116.7 11.9 %collective-permute-start.4 = (bf16[2,160,1024]{2,1,0:T(8,128)(2,1)S(1)}, bf16[2,160,1024]{2,1,0:T(8,128)(2,1)}, u32[]{:S(2)}, u32[]{:S(2)}) collective-permute-start(bf16[2,160,1024]{2,1,0:T(8,128)(2,1)S(1)} %pad_maximum_fusion.own_ref), channel_id=1, source_target_pairs={{0,192},{64,128},{128,64},{192,0},{32,96},{96,32},{160,224},{224,1... | collective-permute-start | bytes 1966088 | tf_op jit(solution)/shard_map/ppermute | solution.py:28
  137.6 16.5 %collective-permute-start.7 = (bf16[4,160,1024]{2,1,0:T(8,128)(2,1)}, bf16[4,160,1024]{2,1,0:T(8,128)(2,1)}, u32[]{:S(2)}, u32[]{:S(2)}) collective-permute-start(bf16[4,160,1024]{2,1,0:T(8,128)(2,1)} %get-tuple-element.42), channel_id=1, source_target_pairs={{0,32},{32,0},{1,33},{33,1},{2,34},{34,2},{3,35},{35,3},{4,36},{36... | collective-permute-start | bytes 3932168 | tf_op jit(solution)/shard_map/ppermute | solution.py:32
  137.7 4.2 %collective-permute-start.6 = (bf16[2,160,1024]{2,1,0:T(8,128)(2,1)}, bf16[2,160,1024]{2,1,0:T(8,128)(2,1)S(1)}, u32[]{:S(2)}, u32[]{:S(2)}) collective-permute-start(bf16[2,160,1024]{2,1,0:T(8,128)(2,1)} %copy-done.9), channel_id=1, source_target_pairs={{0,32},{32,0},{1,33},{33,1},{2,34},{34,2},{3,35},{35,3},{4,36},{36... | collective-permute-start | bytes 1966088 | tf_op jit(solution)/shard_map/ppermute | solution.py:32
  138.2 9.7 %collective-permute-start.5 = (bf16[2,160,1024]{2,1,0:T(8,128)(2,1)}, bf16[2,160,1024]{2,1,0:T(8,128)(2,1)S(1)}, u32[]{:S(2)}, u32[]{:S(2)}) collective-permute-start(bf16[2,160,1024]{2,1,0:T(8,128)(2,1)} %collective-permute-done.4.own_ref), channel_id=1, source_target_pairs={{0,32},{32,0},{1,33},{33,1},{2,34},{34,2},{3,35},{35,3},{4,36},{36... | collective-permute-start | bytes 1966088 | tf_op jit(solution)/shard_map/ppermute | solution.py:32
  155.4 64.5 %all-to-all-start.2 = ((bf16[32,40,896]{2,1,0:T(8,128)(2,1)}), bf16[32,40,896]{2,1,0:T(8,128)(2,1)}, u32[]{:S(2)}, u32[]{:S(2)}) async-start(bf16[32,40,896]{2,1,0:T(8,128)(2,1)} %bitcast.20), calls=%async_computation.2 | async-start | bytes 4587520 | tf_op jit(solution)/shard_map/all_to_all | solution.py:41
  163.9 10.7 %collective-permute-start.8 = (bf16[2,160,1024]{2,1,0:T(8,128)(2,1)S(1)}, bf16[2,160,1024]{2,1,0:T(8,128)(2,1)S(1)}, u32[]{:S(2)}, u32[]{:S(2)}) collective-permute-start(bf16[2,160,1024]{2,1,0:T(8,128)(2,1)S(1)} %add_convert_fusion), channel_id=1, source_target_pairs={{0,64},{64,0},{128,192},{192,128},{32,224},{96,160},{160,96},{224,... | collective-permute-start | bytes 1966088 | tf_op jit(solution)/shard_map/ppermute | solution.py:28
  175.9 8.5 %collective-permute-start.9 = (bf16[160,1024]{1,0:T(8,128)(2,1)S(1)}, bf16[160,1024]{1,0:T(8,128)(2,1)}, u32[]{:S(2)}, u32[]{:S(2)}) collective-permute-start(bf16[160,1024]{1,0:T(8,128)(2,1)S(1)} %fusion.1), channel_id=1, source_target_pairs={{0,192},{64,128},{128,64},{192,0},{32,96},{96,32},{160,224},{224,1... | collective-permute-start | bytes 983048 | tf_op jit(solution)/shard_map/ppermute | solution.py:28
  187.2 7.3 %collective-permute-start.10 = (bf16[160,1024]{1,0:T(8,128)(2,1)}, bf16[160,1024]{1,0:T(8,128)(2,1)S(1)}, u32[]{:S(2)}, u32[]{:S(2)}) collective-permute-start(bf16[160,1024]{1,0:T(8,128)(2,1)} %grad_share.1), channel_id=1, source_target_pairs={{0,64},{64,0},{128,192},{192,128},{32,224},{96,160},{160,96},{224,... | collective-permute-start | bytes 983048 | tf_op jit(solution)/shard_map/ppermute | solution.py:28
  195.5 12.1 %copy-start.10 = (bf16[2,160,1024]{2,1,0:T(8,128)(2,1)}, bf16[2,160,1024]{2,1,0:T(8,128)(2,1)S(1)}, u32[]{:S(2)}) copy-start(bf16[2,160,1024]{2,1,0:T(8,128)(2,1)S(1)} %pad_maximum_fusion.1.own_ref) | copy-start | bytes 1966084
  195.5 12.1 %collective-permute-start.11 = (bf16[2,160,1024]{2,1,0:T(8,128)(2,1)S(1)}, bf16[2,160,1024]{2,1,0:T(8,128)(2,1)S(1)}, u32[]{:S(2)}, u32[]{:S(2)}) collective-permute-start(bf16[2,160,1024]{2,1,0:T(8,128)(2,1)S(1)} %pad_maximum_fusion.1.own_ref), channel_id=1, source_target_pairs={{0,192},{64,128},{128,64},{192,0},{32,96},{96,32},{160,224},{224,1... | collective-permute-start | bytes 1966088 | tf_op jit(solution)/shard_map/ppermute | solution.py:28
  196.0 11.6 %collective-permute-start.13 = (bf16[2,160,1024]{2,1,0:T(8,128)(2,1)S(1)}, bf16[2,160,1024]{2,1,0:T(8,128)(2,1)S(1)}, u32[]{:S(2)}, u32[]{:S(2)}) collective-permute-start(bf16[2,160,1024]{2,1,0:T(8,128)(2,1)S(1)} %pad_maximum_fusion.1.own_ref), channel_id=1, source_target_pairs={{0,32},{32,0},{1,33},{33,1},{2,34},{34,2},{3,35},{35,3},{4,36},{36... | collective-permute-start | bytes 1966088 | tf_op jit(solution)/shard_map/ppermute | solution.py:32
  207.6 6.2 %collective-permute-start.12 = (bf16[2,160,1024]{2,1,0:T(8,128)(2,1)S(1)}, bf16[2,160,1024]{2,1,0:T(8,128)(2,1)S(1)}, u32[]{:S(2)}, u32[]{:S(2)}) collective-permute-start(bf16[2,160,1024]{2,1,0:T(8,128)(2,1)S(1)} %collective-permute-done.11.own_ref), channel_id=1, source_target_pairs={{0,32},{32,0},{1,33},{33,1},{2,34},{34,2},{3,35},{35,3},{4,36},{36... | collective-permute-start | bytes 1966088 | tf_op jit(solution)/shard_map/ppermute | solution.py:32
  219.8 11.8 %copy-start.1 = (bf16[1280,128]{1,0:T(8,128)(2,1)S(1)}, bf16[1280,128]{1,0:T(8,128)(2,1)}, u32[]{:S(2)}) copy-start(bf16[1280,128]{1,0:T(8,128)(2,1)} %get-tuple-element.34.pick_ref) | copy-start | bytes 983044
  219.9 64.8 %all-to-all-start.3 = ((bf16[32,40,896]{2,1,0:T(8,128)(2,1)}), bf16[32,40,896]{2,1,0:T(8,128)(2,1)}, u32[]{:S(2)}, u32[]{:S(2)}) async-start(bf16[32,40,896]{2,1,0:T(8,128)(2,1)} %bitcast.39), calls=%async_computation.3 | async-start | bytes 4587520 | tf_op jit(solution)/shard_map/all_to_all | solution.py:41
  236.9 8.2 %collective-permute-start.14 = (f32[32,128]{1,0:T(8,128)}, f32[32,128]{1,0:T(8,128)}, u32[]{:S(2)}, u32[]{:S(2)}) collective-permute-start(f32[32,128]{1,0:T(8,128)} %gate_terms.1), channel_id=1, source_target_pairs={{0,32},{32,0},{1,33},{33,1},{2,34},{34,2},{3,35},{35,3},{4,36},{36... | collective-permute-start | bytes 49160 | tf_op jit(solution)/shard_map/ppermute | solution.py:32
  246.4 6.6 %collective-permute-start.15 = (f32[32,128]{1,0:T(8,128)}, f32[32,128]{1,0:T(8,128)}, u32[]{:S(2)}, u32[]{:S(2)}) collective-permute-start(f32[32,128]{1,0:T(8,128)} %add.102), channel_id=1, source_target_pairs={{0,64},{64,0},{128,192},{192,128},{32,96},{96,32},{160,224},{224,1... | collective-permute-start | bytes 49160 | tf_op jit(solution)/shard_map/ppermute | solution.py:28
  253.8 4.9 %collective-permute-start.16 = (f32[32,128]{1,0:T(8,128)S(1)}, f32[32,128]{1,0:T(8,128)S(1)}, u32[]{:S(2)}, u32[]{:S(2)}) collective-permute-start(f32[32,128]{1,0:T(8,128)S(1)} %add.103), channel_id=1, source_target_pairs={{0,192},{64,128},{128,64},{192,0},{32,224},{96,160},{160,96},{224,... | collective-permute-start | bytes 49160 | tf_op jit(solution)/shard_map/ppermute | solution.py:28
  (11 other events, 43.8 us)
